TPU v7x, 32 devices: a whole 2x2x4 slice. The times are simulated.
32 devices in a mesh: segment: 4 (over y, x), mp: 8 (over z, core).
Axes of the slice: x: 2, y: 2, z: 4, core: 2. Of those that a mesh axis runs over, the one named last changes fastest.
Arguments:
- noise_init: float32 [2048, 64], P('segment'), may hold values from -6 to 6
- step_noise: float32 [4, 2048, 64], P(None, 'segment'), may hold values from -6 to 6
- assign: int32 [32], P('segment'), may hold values from 0 to 7
- slot_map: int32 [32], replicated, may hold values from 0 to 63, as said below
- prompt_embed: bfloat16 [8, 1536], P('segment', 'mp'), may hold values from -6 to 6
- time_vec: bfloat16 [1536], P('mp'), may hold values from -6 to 6
- w_in: bfloat16 [64, 1536], P('segment', 'mp'), may hold values from -0.75 to 0.75
- ln_gain: bfloat16 [1536], P('mp'), may hold values from 0.099609375 to 1.8984375
- w_up: bfloat16 [1536, 6144], P('segment', 'mp'), may hold values from -0.15625 to 0.15625
- w_down: bfloat16 [6144, 1536], P('mp', 'segment'), may hold values from -0.109375 to 0.109375
- w_out: bfloat16 [1536, 64], P('mp', 'segment'), may hold values from -0.15625 to 0.15625
- conv_in_w: bfloat16 [3, 3, 16, 512], replicated, may hold values from -0.5 to 0.5
- gn_gain: float32 [512], replicated, may hold values from 0.1 to 1.9
- conv_mid_w: bfloat16 [3, 3, 512, 512], replicated, may hold values from -0.09375 to 0.09375
Outputs:
- latents: float32 [2048, 64], P('segment')
- decoded: bfloat16 [64, 2, 128, 512], P('segment', None, 'mp')
Inputs may be any that keep to these rules, and one draw needn't show every extreme that they name: `slot_map`: different samples have different slots. Decoder section d owns slots d * 16 to (d + 1) * 16 - 1; in every draw some section has all of its 16 slots filled, and slots 0 and 63 are used.
All inputs are finite; a program needn't handle non-finite values.
Results may differ from a plain program's by a relative error of at most 0.015.
Values may be sent and summed in bfloat16 or wider, within the bound.
No kernel may reach another device: no remote copies, remote signals or barrier semaphores. Data moves between devices by JAX's collectives and lax.ppermute only.
A program may use at most 64 MiB of HBM per device.

v0:
```python
import functools
import math

import jax
import jax.numpy as jnp
from jax import lax
from jax.experimental import pallas as pl
from jax.experimental.pallas import tpu as pltpu
from jax.sharding import PartitionSpec as P

LAT_CH = 16
VC = 512
GROUPS = 32
STEPS = 4


NOISE_SCALE = 0.5
LATENT_SCALE = 1.0 / 1.5305
EPSILON = 1e-06
GELU_A = math.sqrt(2.0 / math.pi)
GELU_B = GELU_A * 0.044715


def with_halo(cells, sides, width):
    for axis, dim in sides:
        count = lax.axis_size(axis)
        ends = count - 1
        head = lax.slice_in_dim(cells, 0, width, axis=dim)
        tail = lax.slice_in_dim(cells, cells.shape[dim] - width, cells.shape[dim], axis=dim)
        cells = jnp.concatenate(
            [
                lax.ppermute(tail, axis, [(i, (i + 1) % count) for i in range(ends)]),
                cells,
                lax.ppermute(head, axis, [((i + 1) % count, i) for i in range(ends)]),
            ],
            axis=dim,
        )
    return cells


def conv_rows(padded, weight, col_count):
    accumulated = None
    for row_shift in range(3):
        for col_shift in range(3):
            window = padded[:, row_shift : row_shift + 2, col_shift : col_shift + col_count, :]
            product = jnp.einsum(
                "nrcv,vw->nrcw",
                window,
                weight[row_shift, col_shift],
                preferred_element_type=jnp.float32,
            )
            accumulated = product if accumulated is None else accumulated + product
    return accumulated


def decode_tile(latent_tile, tile_cols, image_cols, conv_in_w, gn_gain, conv_mid_w):
    slot_rows = latent_tile.shape[0]
    padded = jnp.pad(latent_tile.astype(jnp.bfloat16), ((0, 0), (1, 1), (0, 0), (0, 0)))
    first_wide = conv_rows(padded, conv_in_w, tile_cols + 2)
    conv_first = first_wide[:, :, 1 : tile_cols + 1, :]
    per_group = VC // GROUPS
    grouped = conv_first.reshape(slot_rows, 2 * tile_cols, GROUPS, per_group)
    group_sum, group_square = lax.psum(
        (jnp.sum(grouped, axis=(1, 3)), jnp.sum(grouped * grouped, axis=(1, 3))), "mp"
    )
    entries = 2 * image_cols * per_group
    average = group_sum / entries
    variance = jnp.maximum(group_square / entries - average * average, 0.0)
    inv_spread = lax.rsqrt(variance + EPSILON)
    col_count = conv_first.shape[2]
    shaped = conv_first.reshape(slot_rows, 2, col_count, GROUPS, per_group)
    shaped = (shaped - average[:, None, None, :, None]) * inv_spread[:, None, None, :, None]
    activated = jax.nn.silu(shaped.reshape(slot_rows, 2, col_count, VC) * gn_gain).astype(
        jnp.bfloat16
    )
    act_wide = with_halo(activated, (("mp", 2),), 1)
    act_padded = jnp.pad(act_wide, ((0, 0), (1, 1), (0, 0), (0, 0)))
    return (conv_first + conv_rows(act_padded, conv_mid_w, tile_cols)).astype(jnp.bfloat16)


def full_front(
    latent_state,
    w_in_full,
    prompt_cond,
    time_full,
    gain_full,
    time_now,
    samples_here,
    tok_sample,
    tok_group,
):
    embedded = jnp.dot(
        latent_state.astype(jnp.bfloat16), w_in_full, preferred_element_type=jnp.float32
    )
    hidden_in = (embedded.reshape(samples_here, tok_sample, -1) + prompt_cond[:, None, :]).reshape(
        tok_group, -1
    ) + time_now * time_full.astype(jnp.float32)
    average = jnp.mean(hidden_in, axis=-1, keepdims=True)
    centered = hidden_in - average
    variance = jnp.mean(centered * centered, axis=-1, keepdims=True)
    normed = (centered * lax.rsqrt(variance + EPSILON) * gain_full.astype(jnp.float32)).astype(
        jnp.bfloat16
    )
    return (hidden_in, normed)


def per_device(
    noise_init,
    step_noise,
    assign,
    slot_map,
    prompt_embed,
    time_vec,
    w_in,
    ln_gain,
    w_up,
    w_down,
    w_out,
    conv_in_w,
    gn_gain,
    conv_mid_w,
):
    mp_count = lax.axis_size("mp")
    mp_index = lax.axis_index("mp")
    segment_index = lax.axis_index("segment")
    w_in_rows, w_up_rows, w_down_cols, w_out_cols, prompt_rows = (
        lax.all_gather(w_in, "segment", axis=0, tiled=True),
        lax.all_gather(w_up, "segment", axis=0, tiled=True),
        lax.all_gather(w_down, "segment", axis=1, tiled=True),
        lax.all_gather(w_out, "segment", axis=1, tiled=True),
        lax.all_gather(prompt_embed, "segment", axis=0, tiled=True),
    )
    samples_here = assign.shape[0]
    tok_group = noise_init.shape[0]
    tok_sample = tok_group // samples_here
    prompt_count = prompt_rows.shape[0]
    choose = (assign[:, None] == jnp.arange(prompt_count, dtype=jnp.int32)[None, :]).astype(
        jnp.bfloat16
    )
    step_size = 1.0 / STEPS
    noise_gain = NOISE_SCALE * math.sqrt(step_size)
    latent_state = noise_init
    w_in_full, prompt_full, w_out_full, time_full, gain_full = (
        lax.all_gather(w_in_rows, "mp", axis=1, tiled=True),
        lax.all_gather(prompt_rows, "mp", axis=1, tiled=True),
        lax.all_gather(w_out_cols, "mp", axis=0, tiled=True),
        lax.all_gather(time_vec, "mp", axis=0, tiled=True),
        lax.all_gather(ln_gain, "mp", axis=0, tiled=True),
    )
    prompt_cond = jnp.dot(choose, prompt_full, preferred_element_type=jnp.float32)
    for step_index in range(STEPS):
        time_now = 1.0 - step_index * step_size
        hidden_in, normed = full_front(
            latent_state,
            w_in_full,
            prompt_cond,
            time_full,
            gain_full,
            time_now,
            samples_here,
            tok_sample,
            tok_group,
        )
        act = jax.nn.gelu(
            jnp.dot(normed, w_up_rows, preferred_element_type=jnp.float32), approximate=True
        ).astype(jnp.bfloat16)
        mlp_out = lax.psum(
            jnp.dot(act, w_down_cols, preferred_element_type=jnp.float32).astype(jnp.bfloat16), "mp"
        ).astype(jnp.float32)
        velocity = jnp.dot(
            (hidden_in + mlp_out).astype(jnp.bfloat16),
            w_out_full,
            preferred_element_type=jnp.float32,
        )
        latent_state = latent_state - step_size * velocity + noise_gain * step_noise[step_index]
    image_cols = 2 * tok_sample
    tile_cols = image_cols // mp_count
    images = (
        latent_state.reshape(samples_here, tok_sample, 2, 2, LAT_CH)
        .transpose(0, 2, 1, 3, 4)
        .reshape(samples_here, 2, image_cols, LAT_CH)
        * LATENT_SCALE
    )
    widened = jnp.pad(images, ((0, 0), (0, 0), (2, 2), (0, 0)))
    latent_tile = lax.dynamic_slice_in_dim(widened, mp_index * tile_cols, tile_cols + 4, 2)
    slot_count = 2 * samples_here
    first_slot = segment_index * slot_count
    slot_ids = first_slot + jnp.arange(slot_count, dtype=jnp.int32)
    slot_picks = (slot_map[None, :] == slot_ids[:, None]).astype(jnp.float32)
    flat_tile = latent_tile.reshape(samples_here, -1)
    owned = jnp.dot(
        slot_picks,
        lax.all_gather(flat_tile, "segment", axis=0, tiled=True),
        preferred_element_type=jnp.float32,
        precision=lax.Precision.HIGHEST,
    )
    decoded = decode_tile(
        owned.reshape(slot_count, 2, tile_cols + 4, LAT_CH),
        tile_cols,
        image_cols,
        conv_in_w,
        gn_gain,
        conv_mid_w,
    )
    return (latent_state, decoded)


ROWS = 48
MIB = 1 << 20


def xor_pieces(value, axis, masks):
    count = lax.axis_size(axis)
    moved = []
    for mask in masks:
        moved.append(lax.ppermute(value, axis, [(i, i ^ mask) for i in range(count)]))
    return moved


def split_three(value):
    high = value.astype(jnp.bfloat16)
    rest = value - high.astype(jnp.float32)
    middle = rest.astype(jnp.bfloat16)
    low = (rest - middle.astype(jnp.float32)).astype(jnp.bfloat16)
    return high, middle, low


def dot32(left, right):
    return jnp.dot(left, right, preferred_element_type=jnp.float32)


def dot_exact(value, exact):
    high, middle, low = split_three(value)
    return dot32(high, exact) + dot32(middle, exact) + dot32(low, exact)


def whole(shape_count):
    return [pl.BlockSpec(memory_space=pltpu.VMEM)] * shape_count


def split_kernel(cfg, *refs):
    segments, quarter = cfg
    w_in_ref, w_out_ref, prompt_ref, time_ref, ln_ref, w_up_ref, w_down_ref, pack_ref = refs[:8]
    outs = refs[8:]
    mine = lax.axis_index("segment")
    rows = w_up_ref.shape[0]
    half = rows // 2
    width = w_in_ref.shape[1]
    in_rows = w_in_ref.shape[0]
    prompt_rows = prompt_ref.shape[0]
    pack_ref[...] = jnp.zeros_like(pack_ref)
    pack_ref[0:in_rows] = w_in_ref[...]
    pack_ref[in_rows : 2 * in_rows] = w_out_ref[...]
    row = lax.broadcasted_iota(jnp.int32, (16, width), 0)
    others = jnp.where(
        row == prompt_rows,
        time_ref[...].astype(jnp.float32).reshape(1, width),
        jnp.where(row == prompt_rows + 1, ln_ref[...].astype(jnp.float32).reshape(1, width), 0.0),
    )
    for index in range(prompt_rows):
        others = jnp.where(
            row == index, prompt_ref[index : index + 1, :].astype(jnp.float32), others
        )
    pack_ref[2 * in_rows : 2 * in_rows + 16] = others.astype(jnp.bfloat16)
    above = rows + half
    for other in range(segments):
        out_ref = outs[other]
        target = lax.bitwise_xor(mine, other)
        start = pl.multiple_of(target * quarter, quarter)
        for index in range(w_down_ref.shape[1] // 128):
            out_ref[above + index * quarter : above + (index + 1) * quarter, :] = w_down_ref[
                pl.ds(start, quarter), index * 128 : (index + 1) * 128
            ]
        for part in range(segments):

            @pl.when(target == part)
            def _():
                block = w_up_ref[:, part * quarter : (part + 1) * quarter]
                out_ref[0:rows, :] = block[:, 0:128]
                tail = block[:, 128:quarter]
                out_ref[rows : rows + half, 0:64] = tail[0:half]
                out_ref[rows : rows + half, 64:128] = tail[half:rows]


def bring(copies):
    for copy in copies:
        copy.start()
    for copy in copies:
        copy.wait()


def table_kernel(cfg, *refs):
    segments, features, slices, latent, prompts = cfg
    own_ref, other_ref, scaled_ref, table_ref, w_out_ref, own, other, canon, sems = refs
    seg = lax.axis_index("segment")
    mp = lax.axis_index("mp")
    bring(
        [
            pltpu.make_async_copy(own_ref, own, sems.at[0]),
            pltpu.make_async_copy(other_ref, other, sems.at[1]),
        ]
    )
    width = own_ref.shape[3]
    stack = segments * ROWS
    in_rows = latent // segments
    prompt_rows = prompts // segments
    column = lax.broadcasted_iota(jnp.int32, (256, stack), 1)
    block = jnp.zeros_like(column)
    for edge in range(1, segments):
        block = block + (column >= edge * ROWS).astype(jnp.int32)
    inner = column - block * ROWS
    source = lax.bitwise_xor(block, seg)
    target = jnp.where(
        inner < in_rows,
        source * in_rows + inner,
        jnp.where(
            inner < 2 * in_rows,
            192 + source * in_rows + inner - in_rows,
            jnp.where(
                inner < 2 * in_rows + prompt_rows,
                64 + source * prompt_rows + inner - 2 * in_rows,
                jnp.where(
                    (block == 0) & (inner < 2 * in_rows + prompt_rows + 2),
                    64 + prompts + inner - 2 * in_rows - prompt_rows,
                    1000,
                ),
            ),
        ),
    )
    row = lax.broadcasted_iota(jnp.int32, (256, stack), 0)
    place = (row == target).astype(jnp.float32).astype(jnp.bfloat16)
    total = jnp.zeros((128, 1), jnp.float32)
    for index in range(slices):
        ref = own if index % 2 == 0 else other
        where_to = lax.bitwise_xor(mp, index)
        both = dot32(place, ref[index // 2].reshape(stack, width))
        canon[where_to] = both[0:128]
        table_ref[where_to] = both[0:80].astype(jnp.bfloat16)
        start = pl.multiple_of(where_to * width, width)
        w_out_ref[pl.ds(start, width), :] = jnp.transpose(both[128:256]).astype(jnp.bfloat16)
        total = total + jnp.sum(both[0:128], axis=1, keepdims=True)
    average = total / features
    for index in range(slices):
        part = canon[index]
        scaled = (part - average) * part[64 + prompts + 1 : 64 + prompts + 2, :]
        high = scaled.astype(jnp.bfloat16)
        scaled_ref[index, 0:128] = high
        scaled_ref[index, 128:256] = (scaled - high.astype(jnp.float32)).astype(jnp.bfloat16)


def combine_kernel(cfg, *refs):
    segments, slices, width, quarter = cfg
    scaled_ref, w_out_ref = refs[:2]
    sources = refs[2 : 2 + segments]
    piece_ref = refs[2 + segments]
    blocks, sems = refs[3 + segments :]
    seg = lax.axis_index("segment")
    bring(
        [pltpu.make_async_copy(sources[i], blocks.at[i], sems.at[i]) for i in range(segments)]
    )
    per_segment = slices // segments
    rows = per_segment * width
    above = rows + rows // 2
    main = jnp.zeros((128, 128), jnp.float32)
    tail = jnp.zeros((128, 128), jnp.float32)
    down = jnp.zeros((quarter, 128), jnp.float32)
    for other in range(segments):
        source_seg = lax.bitwise_xor(seg, other)
        for unit in range(per_segment):
            both = scaled_ref[source_seg * per_segment + unit]
            product = dot32(both, blocks[other, unit * width : (unit + 1) * width, :])
            main = main + product[0:128] + product[128:256]
            product = dot32(both, blocks[other, rows:above, :])
            product = product[0:128] + product[128:256]
            tail = tail + (product if unit == 0 else pltpu.roll(product, 64, 1))
        for index in range(rows // 128):
            start = pl.multiple_of(source_seg * rows + index * 128, 128)
            at = above + index * quarter
            down = down + dot32(
                blocks[other, at : at + quarter, :], w_out_ref[pl.ds(start, 128), :]
            )
    lane = lax.broadcasted_iota(jnp.int32, (1, 128), 1)
    down = 0.5 * down
    piece_ref[0:128, :] = jnp.where(lane < 64, jnp.transpose(main), down[0:128]).astype(
        jnp.bfloat16
    )
    piece_ref[128:192, :] = jnp.where(
        lane < 64, jnp.transpose(tail)[0:64], down[128:192]
    ).astype(jnp.bfloat16)
    piece_ref[192:208, :] = main[64:80].astype(jnp.bfloat16)
    piece_ref[208:224, :] = tail[64:80].astype(jnp.bfloat16)


def loop_kernel(cfg, *refs):
    features, slices, prompts, chunk = cfg
    assign_ref, noise_ref, step_ref, table_ref, w_out_ref = refs[:5]
    pieces = refs[5:-9]
    result_ref, state, steps, const, hidden, weights, extras, turned, sems = refs[-9:]
    mp = lax.axis_index("mp")
    tokens = state.shape[0]
    width = table_ref.shape[2]
    pair = lax.shift_right_logical(mp, 1)
    odd = lax.bitwise_and(mp, 1)
    copies = []
    for i, ref in enumerate(pieces):
        copies.append(
            pltpu.make_async_copy(ref.at[:, 0:192, :], weights.at[i], sems.at[2 * i])
        )
        copies.append(
            pltpu.make_async_copy(ref.at[:, 192:224, :], extras.at[i], sems.at[2 * i + 1])
        )
    for copy in copies:
        copy.start()
    prompt = assign_ref[mp]
    lane = lax.broadcasted_iota(jnp.int32, (1, 128), 1)
    lanes_from = pl.multiple_of(pair * 128, 128)
    rows_from = pl.multiple_of(odd * tokens, tokens)
    steps[...] = jnp.zeros_like(steps)
    state[...] = jnp.zeros_like(state)
    turned[...] = jnp.transpose(noise_ref[:, pl.ds(lanes_from, 128)])
    state[:, 0:64] = turned[pl.ds(rows_from, tokens), :]
    for index in range(STEPS):
        turned[...] = jnp.transpose(step_ref[index, :, pl.ds(lanes_from, 128)])
        steps[index, :, 0:64] = turned[pl.ds(rows_from, tokens), :]
    sixteen = lax.broadcasted_iota(jnp.int32, (16, 1), 0)
    pick = (sixteen == prompt).astype(jnp.float32)
    timing = (sixteen == prompts).astype(jnp.float32)
    for copy in copies:
        copy.wait()
    flat = [(i, j) for i in range(len(pieces)) for j in range(weights.shape[1])]
    for two in range(len(flat) // 2):
        e = [
            extras[flat[two * 2 + h][0], flat[two * 2 + h][1], 16 * i : 16 * i + 16, :].astype(
                jnp.float32
            )
            for h in range(2)
            for i in range(2)
        ]
        moved = pltpu.roll(e[2], 64, 1)
        lanes = [
            e[0],
            jnp.where(lane < 64, e[1], moved),
            jnp.where(lane < 64, moved, pltpu.roll(e[3], 64, 1)),
        ]
        for third in range(3):
            at = two * 384 + third * 128
            const[0:1, at : at + 128] = jnp.sum(pick * lanes[third], axis=0, keepdims=True)
            const[1:2, at : at + 128] = jnp.sum(timing * lanes[third], axis=0, keepdims=True)
    count = len(flat) * 192
    step_size = 1.0 / STEPS
    noise_gain = NOISE_SCALE * math.sqrt(step_size)

    def one_step(step, carry):
        time_now = 1.0 - step.astype(jnp.float32) * step_size
        now = state[...]
        operand = now.astype(jnp.bfloat16)
        narrow = operand[:, 0:64]
        weight = pick + time_now * timing
        total = jnp.zeros((tokens, 1), jnp.float32)
        for index in range(slices):
            base = jnp.sum(
                table_ref[index, 64:80, :].astype(jnp.float32) * weight, axis=0, keepdims=True
            )
            value = dot32(narrow, table_ref[index, 0:64, :]) + base
            hidden[index] = value
            total = total + jnp.sum(value, axis=1, keepdims=True)
        average = total / features
        square = jnp.zeros((tokens, 1), jnp.float32)
        velocity = jnp.zeros((tokens, 128), jnp.float32)
        for index in range(slices):
            value = hidden[index]
            centered = value - average
            square = square + jnp.sum(centered * centered, axis=1, keepdims=True)
            velocity = velocity + dot32(
                value.astype(jnp.bfloat16), w_out_ref[index * width : (index + 1) * width, :]
            )
        spread = lax.rsqrt(square / features + EPSILON)
        per_block = weights.shape[1] * 192
        for at in range(0, count, chunk):
            block = at // per_block
            inside = (at % per_block) // 192
            part = weights[block, inside : inside + chunk // 192].reshape(chunk, 128)
            shift = const[0:1, at : at + chunk] + time_now * const[1:2, at : at + chunk]
            pre = lax.dot_general(
                operand, part, (((1,), (1,)), ((), ())), preferred_element_type=jnp.float32
            )
            pre = (pre + shift) * spread
            inner = pre * (GELU_A + GELU_B * (pre * pre))
            act = (pre + pre * jnp.tanh(inner)).astype(jnp.bfloat16)
            velocity = velocity + dot32(act, part)
        moved = pltpu.roll(velocity, 64, 1)
        fresh = now - step_size * moved + noise_gain * steps[step]
        state[...] = jnp.where(lane < 64, fresh, 0.0)
        return carry

    lax.fori_loop(0, STEPS, one_step, 0)
    half = tokens // 2
    result_ref[...] = state[0:half] + pltpu.roll(state[half:tokens], 64, 1)


def patches_of(piece):
    lane = lax.broadcasted_iota(jnp.int32, (1, 128), 1)
    low = jnp.where(lane < 64, piece, 0.0)
    high = jnp.where(lane < 64, pltpu.roll(piece, 64, 1), 0.0)
    image = jnp.concatenate([low, high], axis=0) * LATENT_SCALE
    tokens = image.shape[0]
    row = lax.broadcasted_iota(jnp.int32, (tokens, 128), 0)
    before = jnp.where(row == 0, 0.0, pltpu.roll(image, 1, 0))
    after = jnp.where(row == tokens - 1, 0.0, pltpu.roll(image, tokens - 1, 0))
    odd = lax.bitwise_and(lax.shift_right_logical(lane, 4), 1) == 1
    beside = pltpu.roll(jnp.where(odd, before, after), 64, 1)
    return (image + beside).astype(jnp.bfloat16)


def decode_kernel(cfg, *refs):
    _, mp_count, samples_here, image_cols = cfg
    (map_ref, own_ref, other_ref, conv_in_ref, gain_ref, conv_mid_any, latents_ref, out_ref,
     table, received, patches, front, sums, squares, means, act, center, lines, conv_mid_ref,
     sems) = refs
    seg = lax.axis_index("segment")
    mp = lax.axis_index("mp")
    slots = out_ref.shape[0]
    half_pieces = own_ref.shape[0]
    pieces = 2 * half_pieces
    tokens = 2 * own_ref.shape[1]
    tile = out_ref.shape[2]
    tile_tokens = tile // 2
    lats = LAT_CH
    weight_copy = pltpu.make_async_copy(conv_mid_any, conv_mid_ref, sems.at[0])
    weight_copy.start()
    arrivals = [
        pltpu.make_async_copy(own_ref, received.at[0:half_pieces], sems.at[1]),
        pltpu.make_async_copy(other_ref, received.at[half_pieces:pieces], sems.at[2]),
    ]
    for copy in arrivals:
        copy.start()
    for slot in range(slots):
        table[slot] = pieces
    z_count = mp_count // 2
    for sample in range(map_ref.shape[0]):
        owner = lax.bitwise_xor(mp, sample % samples_here)
        place = (
            lax.bitwise_and(owner, 1) * half_pieces
            + lax.bitwise_xor(seg, sample // samples_here) * z_count
            + lax.shift_right_logical(owner, 1)
        )
        relative = map_ref[sample] - seg * slots

        @pl.when((relative >= 0) & (relative < slots))
        def _():
            table[relative] = place

    received[pieces] = jnp.zeros_like(received[0])
    front[...] = jnp.zeros_like(front)
    for group in range(8):
        if group < 4:
            row_in, offset = group // 2, group % 2
        else:
            row_in, offset = (group - 4) // 2, 2 if group % 2 == 0 else -1
        for out in range(4):
            row_out, col_out = out // 2, out % 2
            i, j = row_in - row_out + 1, offset - col_out + 1
            if 0 <= j <= 2:
                front[group * lats : (group + 1) * lats, out * VC : (out + 1) * VC] = (
                    conv_in_ref[i, j]
                )
    for copy in arrivals:
        copy.wait()
    for slot in range(slots):
        patch = patches_of(received[table[slot]])
        patches[slot] = patch
        sums[slot : slot + 1, :] = jnp.sum(patch.astype(jnp.float32), axis=0, keepdims=True)
    lane = lax.broadcasted_iota(jnp.int32, (1, 128), 1)
    half = tokens // 2
    for core in range(2):
        for line in range(z_count):
            piece = received[core * half_pieces + line]
            to = lax.bitwise_xor(lax.shift_right_logical(mp, 1), line)
            at = lax.bitwise_xor(lax.bitwise_and(mp, 1), core) * tokens
            lines[to, pl.ds(pl.multiple_of(at, tokens), half), :] = piece
            lines[to, pl.ds(pl.multiple_of(at + half, half), half), :] = pltpu.roll(piece, 64, 1)
    for line in range(z_count):
        block = jnp.transpose(lines[line])
        latents_ref[:, line * 128 : (line + 1) * 128] = block[0:64]
    per_group = VC // GROUPS
    entries = 2 * image_cols * per_group
    row_c = lax.broadcasted_iota(jnp.int32, (VC, VC), 0) // per_group
    col_c = lax.broadcasted_iota(jnp.int32, (VC, VC), 1) // per_group
    same = (row_c == col_c).astype(jnp.float32).astype(jnp.bfloat16)
    wide = dot_exact(sums[...], front[...])
    wide = wide[:, 0:VC] + wide[:, VC : 2 * VC] + wide[:, 2 * VC : 3 * VC] + wide[:, 3 * VC :]
    average = dot_exact(wide, same) / entries
    means[...] = average

    def one_slot(slot, carry):
        patch = patches[slot]
        mean = means[pl.ds(slot, 1), :]
        collected = None
        for out in range(4):
            value = dot32(patch, front[:, out * VC : (out + 1) * VC]) - mean
            value = value * value
            part = value[0:8]
            for at in range(8, tokens, 8):
                part = part + value[at : at + 8]
            collected = part if collected is None else collected + part
        squares[pl.ds(slot, 1), :] = jnp.sum(collected, axis=0, keepdims=True)
        return carry

    lax.fori_loop(0, slots, one_slot, 0)
    variance = dot_exact(squares[...], same) / entries
    spread = lax.rsqrt(variance + EPSILON)
    gain = gain_ref[...]
    count = (tile_tokens + 2) * slots
    row_t = lax.broadcasted_iota(jnp.int32, (count, 1), 0)
    token = row_t // slots
    slot_of = row_t - token * slots
    token = token + mp * tile_tokens - 1
    inside = (token >= 0) & (token < tokens)
    wanted = jnp.where(inside, slot_of * tokens + token, -1)
    column = lax.broadcasted_iota(jnp.int32, (count, slots * tokens), 1)
    pick = (column == wanted).astype(jnp.float32).astype(jnp.bfloat16)
    rows = dot32(pick, patches[...].reshape(slots * tokens, 128)).astype(jnp.bfloat16)
    for out in range(4):
        row_out, col_out = out // 2, out % 2
        value = dot32(rows, front[:, out * VC : (out + 1) * VC])
        for t in range(tile_tokens + 2):
            part = value[t * slots : (t + 1) * slots]
            at = (2 * t + col_out) * slots
            if 1 <= t <= tile_tokens:
                center[row_out, at - 2 * slots : at - slots, :] = part
            scaled = (part - average) * spread * gain
            silu = 0.5 * scaled * (1.0 + jnp.tanh(0.5 * scaled))
            if t == 0:
                silu = jnp.where(mp == 0, 0.0, silu)
            if t == tile_tokens + 1:
                silu = jnp.where(mp == mp_count - 1, 0.0, silu)
            act[row_out, at : at + slots, :] = silu.astype(jnp.bfloat16)
    weight_copy.wait()
    size = tile * slots
    row_p = lax.broadcasted_iota(jnp.int32, (size, size), 0)
    col_p = lax.broadcasted_iota(jnp.int32, (size, size), 1)
    slot_p = row_p // tile
    swap = (col_p == (row_p - slot_p * tile) * slots + slot_p).astype(jnp.float32)
    swap = swap.astype(jnp.bfloat16)
    for row_out in range(2):
        total = center[row_out]
        for row_in in range(2):
            for shift in range(3):
                at = (1 + shift) * slots
                total = total + dot32(
                    act[row_in, at : at + size, :], conv_mid_ref[row_in - row_out + 1, shift]
                )
        ordered = dot32(swap, total.astype(jnp.bfloat16)).astype(jnp.bfloat16)
        out_ref[:, row_out, :, :] = ordered.reshape(slots, tile, VC)


def per_device_fast(
    noise_init,
    step_noise,
    assign,
    slot_map,
    prompt_embed,
    time_vec,
    w_in,
    ln_gain,
    w_up,
    w_down,
    w_out,
    conv_in_w,
    gn_gain,
    conv_mid_w,
):
    segments = lax.axis_size("segment")
    mp_count = lax.axis_size("mp")
    around = range(1, segments)
    along = range(2, mp_count, 2)
    width = w_in.shape[1]
    features = width * mp_count
    latent = w_in.shape[0] * segments
    prompts = prompt_embed.shape[0] * segments
    samples_here = assign.shape[0]
    tok_group = noise_init.shape[0]
    tokens = tok_group // mp_count
    hidden = w_up.shape[1]
    quarter = hidden // segments
    bf16, f32 = jnp.bfloat16, jnp.float32
    any_space = pl.BlockSpec(memory_space=pl.ANY)
    smem = pl.BlockSpec(memory_space=pltpu.SMEM)
    joint = w_up.shape[0] * 3 // 2 + quarter * (w_down.shape[1] // 128)
    pack, *split = pl.pallas_call(
        functools.partial(split_kernel, (segments, quarter)),
        out_shape=[jax.ShapeDtypeStruct((ROWS, width), bf16)]
        + [jax.ShapeDtypeStruct((joint, 128), bf16)] * segments,
        in_specs=whole(7),
        out_specs=whole(1 + segments),
        name="split_weights",
    )(w_in, w_out.T, prompt_embed, time_vec, ln_gain, w_up, w_down)
    table = jnp.stack([pack] + xor_pieces(pack, "segment", around))
    sources = [split[0]]
    for other in around:
        sources += xor_pieces(split[other], "segment", [other])
    table = jnp.stack([table] + xor_pieces(table, "mp", along))
    (table_other,) = xor_pieces(table, "mp", [1])
    scaled, tables, w_out_all = pl.pallas_call(
        functools.partial(table_kernel, (segments, features, mp_count, latent, prompts)),
        out_shape=[
            jax.ShapeDtypeStruct((mp_count, 256, width), bf16),
            jax.ShapeDtypeStruct((mp_count, 80, width), bf16),
            jax.ShapeDtypeStruct((features, 128), bf16),
        ],
        in_specs=[any_space] * 2,
        out_specs=whole(3),
        scratch_shapes=[
            pltpu.VMEM(table.shape, bf16),
            pltpu.VMEM(table.shape, bf16),
            pltpu.VMEM((mp_count, 128, width), f32),
            pltpu.SemaphoreType.DMA((2,)),
        ],
        compiler_params=pltpu.CompilerParams(vmem_limit_bytes=16 * MIB),
        name="order_tables",
    )(table, table_other)
    piece = pl.pallas_call(
        functools.partial(combine_kernel, (segments, mp_count, width, quarter)),
        out_shape=jax.ShapeDtypeStruct((quarter + 32, 128), bf16),
        in_specs=whole(2) + [any_space] * segments,
        out_specs=whole(1)[0],
        scratch_shapes=[
            pltpu.VMEM((segments, joint, 128), bf16),
            pltpu.SemaphoreType.DMA((segments,)),
        ],
        compiler_params=pltpu.CompilerParams(vmem_limit_bytes=16 * MIB),
        name="combine_weights",
    )(scaled, w_out_all, *sources)
    line = jnp.stack([piece] + xor_pieces(piece, "mp", along))
    plane = [line]
    for other in around:
        plane += xor_pieces(line, "segment", [other])
    plane = plane + [xor_pieces(block, "mp", [1])[0] for block in plane]
    half = mp_count // 2
    result = pl.pallas_call(
        functools.partial(loop_kernel, (features, mp_count, prompts, 384)),
        out_shape=jax.ShapeDtypeStruct((tokens // 2, 128), f32),
        in_specs=[smem] + whole(4) + [any_space] * len(plane),
        out_specs=whole(1)[0],
        scratch_shapes=[
            pltpu.VMEM((tokens, 128), f32),
            pltpu.VMEM((STEPS, tokens, 128), f32),
            pltpu.VMEM((8, len(plane) * half * quarter), f32),
            pltpu.VMEM((mp_count, tokens, width), f32),
            pltpu.VMEM((len(plane), half, quarter, 128), bf16),
            pltpu.VMEM((len(plane), half, 32, 128), bf16),
            pltpu.VMEM((128, 64), f32),
            pltpu.SemaphoreType.DMA((2 * len(plane),)),
        ],
        compiler_params=pltpu.CompilerParams(vmem_limit_bytes=24 * MIB),
        name="denoise",
    )(assign, noise_init.T, step_noise.transpose(0, 2, 1), tables, w_out_all, *plane)
    image = jnp.stack([result] + xor_pieces(result, "mp", along))
    image = jnp.concatenate([image] + xor_pieces(image, "segment", around), axis=0)
    (image_other,) = xor_pieces(image, "mp", [1])
    image_cols = 2 * tokens
    tile = image_cols // mp_count
    slots = 2 * samples_here
    pieces = segments * mp_count
    latents, decoded = pl.pallas_call(
        functools.partial(decode_kernel, (segments, mp_count, samples_here, image_cols)),
        out_shape=[
            jax.ShapeDtypeStruct((64, tok_group), f32),
            jax.ShapeDtypeStruct((slots, 2, tile, VC), bf16),
        ],
        in_specs=[smem, any_space, any_space] + whole(2) + [any_space],
        out_specs=whole(2),
        scratch_shapes=[
            pltpu.SMEM((slots,), jnp.int32),
            pltpu.VMEM((pieces + 1, tokens // 2, 128), f32),
            pltpu.VMEM((slots, tokens, 128), bf16),
            pltpu.VMEM((128, 4 * VC), bf16),
            pltpu.VMEM((slots, 128), f32),
            pltpu.VMEM((slots, VC), f32),
            pltpu.VMEM((slots, VC), f32),
            pltpu.VMEM((2, (tile + 4) * slots, VC), bf16),
            pltpu.VMEM((2, tile * slots, VC), f32),
            pltpu.VMEM((half, 128, 128), f32),
            pltpu.VMEM(conv_mid_w.shape, bf16),
            pltpu.SemaphoreType.DMA((3,)),
        ],
        compiler_params=pltpu.CompilerParams(vmem_limit_bytes=40 * MIB),
        name="decode",
    )(slot_map, image, image_other, conv_in_w, gn_gain[None, :], conv_mid_w)
    return latents.T, decoded


def choose(*args):
    segments, mp_count = lax.axis_size("segment"), lax.axis_size("mp")
    noise, assign, prompt, w_in, w_up = (args[i].shape for i in (0, 2, 4, 6, 8))
    ready = (
        mp_count == 2 * segments == 8
        and noise[0] // mp_count == noise[0] // assign[0] == 64
        and w_up[1] // segments == w_in[1] == 192
        and w_in[0] * segments == noise[1] == 64
        and prompt[0] * segments <= 8
    )
    return (per_device_fast if ready else per_device)(*args)


def solution(mesh):
    return jax.shard_map(
        choose,
        mesh=mesh,
        in_specs=(
            P("segment", None),
            P(None, "segment", None),
            P("segment"),
            P(),
            P("segment", "mp"),
            P("mp"),
            P("segment", "mp"),
            P("mp"),
            P("segment", "mp"),
            P("mp", "segment"),
            P("mp", "segment"),
            P(),
            P(),
            P(),
        ),
        out_specs=(P("segment", None), P("segment", None, "mp", None)),
        check_vma=False,
    )
```

profile of v0, /device:TPU:1, one launch (start us, length us, event | category | flops | bytes accessed | tf_op | source)
XLA Modules:
  0.0 103.3 jit_solution(12139131913465761407)
XLA Ops:
  0.7 3.0 %split_weights.1 = (bf16[48,192]{1,0:T(8,128)(2,1)}, bf16[1152,128]{1,0:T(8,128)(2,1)}, bf16[1152,128]{1,0:T(8,128)(2,1)}, bf16[1152,128]{1,0:T(8,128)(2,1)}, bf16[1152,128]{1,0:T(8,128)(2,1)}) custom-call(bf16[16,192]{1,0:T(8,128)(2,1)} %refs_0_.3, bf16[16,192]{1,0:T(8,128)(2,1)} %bitcast.44, bf16[2,192]{1,0:T(2,128)(2,1)} %refs_2_.1, ...), custom_call_target="tpu_custom_call" | custom-call | tf_op jit(solution)/shard_map/split_weights/pallas_call | solution.py:690
  3.7 3.0 %collective-permute-start.2 = (bf16[48,192]{1,0:T(8,128)(2,1)}, bf16[48,192]{1,0:T(8,128)(2,1)S(1)}, u32[]{:S(2)}, u32[]{:S(2)}) collective-permute-start(bf16[48,192]{1,0:T(8,128)(2,1)} %get-tuple-element.12), channel_id=1, source_target_pairs={{0,24},{8,16},{16,8},{24,0},{1,25},{9,17},{17,9},{25,1},{2,26},{10... | collective-permute-start | bytes 55304 | tf_op jit(solution)/shard_map/ppermute | solution.py:216
  6.7 0.2 collective-permute-start.1
  6.9 0.1 collective-permute-start
  7.0 1.1 %collective-permute-done.2 = bf16[48,192]{1,0:T(8,128)(2,1)S(1)} collective-permute-done((bf16[48,192]{1,0:T(8,128)(2,1)}, bf16[48,192]{1,0:T(8,128)(2,1)S(1)}, u32[]{:S(2)}, u32[]{:S(2)}) %collective-permute-start.2) | collective-permute-done | bytes 18464 | tf_op jit(solution)/shard_map/ppermute | solution.py:216
  8.1 1.5 %collective-permute-done.1 = bf16[48,192]{1,0:T(8,128)(2,1)S(1)} collective-permute-done((bf16[48,192]{1,0:T(8,128)(2,1)}, bf16[48,192]{1,0:T(8,128)(2,1)S(1)}, u32[]{:S(2)}, u32[]{:S(2)}) %collective-permute-start.1) | collective-permute-done | bytes 18464 | tf_op jit(solution)/shard_map/ppermute | solution.py:216
  9.5 0.2 collective-permute-done
  9.8 0.8 fusion
  10.5 2.4 %collective-permute-start.4 = (bf16[4,48,192]{2,1,0:T(8,128)(2,1)S(1)}, bf16[4,48,192]{2,1,0:T(8,128)(2,1)S(1)}, u32[]{:S(2)}, u32[]{:S(2)}) collective-permute-start(bf16[4,48,192]{2,1,0:T(8,128)(2,1)S(1)} %get-tuple-element.23), channel_id=1, source_target_pairs={{0,4},{1,5},{2,6},{3,7},{4,0},{5,1},{6,2},{7,3},{8,12},{9,13},{10,... | collective-permute-start | bytes 221192 | tf_op jit(solution)/shard_map/ppermute | solution.py:216
  12.9 1.3 %collective-permute-start.3 = (bf16[4,48,192]{2,1,0:T(8,128)(2,1)S(1)}, bf16[4,48,192]{2,1,0:T(8,128)(2,1)S(1)}, u32[]{:S(2)}, u32[]{:S(2)}) collective-permute-start(bf16[4,48,192]{2,1,0:T(8,128)(2,1)S(1)} %get-tuple-element.23), channel_id=1, source_target_pairs={{0,2},{1,3},{2,0},{3,1},{4,6},{5,7},{6,4},{7,5},{8,10},{9,11},{10,... | collective-permute-start | bytes 221192 | tf_op jit(solution)/shard_map/ppermute | solution.py:216
  14.2 0.3 collective-permute-start.7
  14.5 0.5 collective-permute-done.4
  15.0 1.4 %collective-permute-done.3 = bf16[4,48,192]{2,1,0:T(8,128)(2,1)S(1)} collective-permute-done((bf16[4,48,192]{2,1,0:T(8,128)(2,1)S(1)}, bf16[4,48,192]{2,1,0:T(8,128)(2,1)S(1)}, u32[]{:S(2)}, u32[]{:S(2)}) %collective-permute-start.3) | collective-permute-done | bytes 73760 | tf_op jit(solution)/shard_map/ppermute | solution.py:216
  16.4 4.2 %collective-permute-done.5 = bf16[4,48,192]{2,1,0:T(8,128)(2,1)S(1)} collective-permute-done((bf16[4,48,192]{2,1,0:T(8,128)(2,1)S(1)}, bf16[4,48,192]{2,1,0:T(8,128)(2,1)S(1)}, u32[]{:S(2)}, u32[]{:S(2)}) %collective-permute-start.5) | collective-permute-done | bytes 73760 | tf_op jit(solution)/shard_map/ppermute | solution.py:216
  20.7 3.1 %collective-permute-start.6 = (bf16[4,4,48,192]{3,2,1,0:T(8,128)(2,1)S(1)}, bf16[4,4,48,192]{3,2,1,0:T(8,128)(2,1)S(1)}, u32[]{:S(2)}, u32[]{:S(2)}) collective-permute-start(bf16[4,4,48,192]{3,2,1,0:T(8,128)(2,1)S(1)} %pad_maximum_fusion.refs_0_), channel_id=1, source_target_pairs={{0,1},{1,0},{2,3},{3,2},{4,5},{5,4},{6,7},{7,6},{8,9},{9,8},{10,11... | collective-permute-start | bytes 884744 | tf_op jit(solution)/shard_map/ppermute | solution.py:216
  23.7 1.3 %collective-permute-start.8 = (bf16[1152,128]{1,0:T(8,128)(2,1)}, bf16[1152,128]{1,0:T(8,128)(2,1)S(1)}, u32[]{:S(2)}, u32[]{:S(2)}) collective-permute-start(bf16[1152,128]{1,0:T(8,128)(2,1)} %get-tuple-element.18), channel_id=1, source_target_pairs={{0,16},{8,24},{16,0},{24,8},{1,17},{9,25},{17,1},{25,9},{2,18},{10... | collective-permute-start | bytes 884744 | tf_op jit(solution)/shard_map/ppermute | solution.py:216
  25.1 0.1 collective-permute-start.9
  25.2 1.3 %order_tables.1 = (bf16[8,256,192]{2,1,0:T(8,128)(2,1)S(1)}, bf16[8,80,192]{2,1,0:T(8,128)(2,1)S(1)}, bf16[1536,128]{1,0:T(8,128)(2,1)S(1)}) custom-call(bf16[4,4,48,192]{3,2,1,0:T(8,128)(2,1)S(1)} %pad_maximum_fusion.refs_0_, bf16[4,4,48,192]{3,2,1,0:T(8,128)(2,1)S(1)} %collective-permute-done.6.refs_1_), custom_call_target="tpu_custom_call" | custom-call | tf_op jit(solution)/shard_map/order_tables/pallas_call | solution.py:704
  26.5 12.3 %collective-permute-done.8.refs_4_ = bf16[1152,128]{1,0:T(8,128)(2,1)S(1)} collective-permute-done((bf16[1152,128]{1,0:T(8,128)(2,1)}, bf16[1152,128]{1,0:T(8,128)(2,1)S(1)}, u32[]{:S(2)}, u32[]{:S(2)}) %collective-permute-start.8) | collective-permute-done | bytes 294944 | tf_op jit(solution)/shard_map/ppermute | solution.py:216
  38.8 1.0 copy-done.2
  39.7 1.2 %combine_weights.1 = bf16[224,128]{1,0:T(8,128)(2,1)S(1)} custom-call(bf16[8,256,192]{2,1,0:T(8,128)(2,1)S(1)} %get-tuple-element.15.refs_0_, bf16[1536,128]{1,0:T(8,128)(2,1)S(1)} %get-tuple-element.14.refs_1_.refs_4_, bf16[1152,128]{1,0:T(8,128)(2,1)S(1)} %copy-done.2, bf16[1152,128]{1,0:T(8,128)(2,1)S(1)} %collective-permute-done.7.refs_3_, ...), custom_call_target="tpu_custom_call" | custom-call | tf_op jit(solution)/shard_map/combine_weights/pallas_call | solution.py:722
  41.0 1.8 %collective-permute-start.12 = (bf16[224,128]{1,0:T(8,128)(2,1)S(1)}, bf16[224,128]{1,0:T(8,128)(2,1)S(1)}, u32[]{:S(2)}, u32[]{:S(2)}) collective-permute-start(bf16[224,128]{1,0:T(8,128)(2,1)S(1)} %combine_weights.1), channel_id=1, source_target_pairs={{0,6},{1,7},{2,4},{3,5},{4,2},{5,3},{6,0},{7,1},{8,14},{9,15},{10,... | collective-permute-start | bytes 172040 | tf_op jit(solution)/shard_map/ppermute | solution.py:216
  42.8 0.2 collective-permute-start.11
  43.0 1.6 %collective-permute-start.10 = (bf16[224,128]{1,0:T(8,128)(2,1)S(1)}, bf16[224,128]{1,0:T(8,128)(2,1)S(1)}, u32[]{:S(2)}, u32[]{:S(2)}) collective-permute-start(bf16[224,128]{1,0:T(8,128)(2,1)S(1)} %combine_weights.1), channel_id=1, source_target_pairs={{0,2},{1,3},{2,0},{3,1},{4,6},{5,7},{6,4},{7,5},{8,10},{9,11},{10,... | collective-permute-start | bytes 172040 | tf_op jit(solution)/shard_map/ppermute | solution.py:216
  44.6 1.4 %collective-permute-done.12 = bf16[224,128]{1,0:T(8,128)(2,1)S(1)} collective-permute-done((bf16[224,128]{1,0:T(8,128)(2,1)S(1)}, bf16[224,128]{1,0:T(8,128)(2,1)S(1)}, u32[]{:S(2)}, u32[]{:S(2)}) %collective-permute-start.12) | collective-permute-done | bytes 57376 | tf_op jit(solution)/shard_map/ppermute | solution.py:216
  46.0 3.2 %collective-permute-done.11 = bf16[224,128]{1,0:T(8,128)(2,1)S(1)} collective-permute-done((bf16[224,128]{1,0:T(8,128)(2,1)S(1)}, bf16[224,128]{1,0:T(8,128)(2,1)S(1)}, u32[]{:S(2)}, u32[]{:S(2)}) %collective-permute-start.11) | collective-permute-done | bytes 57376 | tf_op jit(solution)/shard_map/ppermute | solution.py:216
  49.3 1.5 %collective-permute-start.15 = (bf16[4,224,128]{2,1,0:T(8,128)(2,1)S(1)}, bf16[4,224,128]{2,1,0:T(8,128)(2,1)S(1)}, u32[]{:S(2)}, u32[]{:S(2)}) collective-permute-start(bf16[4,224,128]{2,1,0:T(8,128)(2,1)S(1)} %pad_maximum_fusion.1.refs_5_), channel_id=1, source_target_pairs={{0,24},{8,16},{16,8},{24,0},{1,25},{9,17},{17,9},{25,1},{2,26},{10... | collective-permute-start | bytes 688136 | tf_op jit(solution)/shard_map/ppermute | solution.py:216
  50.9 1.1 %collective-permute-start.13 = (bf16[4,224,128]{2,1,0:T(8,128)(2,1)S(1)}, bf16[4,224,128]{2,1,0:T(8,128)(2,1)S(1)}, u32[]{:S(2)}, u32[]{:S(2)}) collective-permute-start(bf16[4,224,128]{2,1,0:T(8,128)(2,1)S(1)} %pad_maximum_fusion.1.refs_5_), channel_id=1, source_target_pairs={{0,8},{8,0},{16,24},{24,16},{1,9},{9,1},{17,25},{25,17},{2,10},{10... | collective-permute-start | bytes 688136 | tf_op jit(solution)/shard_map/ppermute | solution.py:216
  52.0 1.5 %collective-permute-start.16 = (bf16[4,224,128]{2,1,0:T(8,128)(2,1)S(1)}, bf16[4,224,128]{2,1,0:T(8,128)(2,1)S(1)}, u32[]{:S(2)}, u32[]{:S(2)}) collective-permute-start(bf16[4,224,128]{2,1,0:T(8,128)(2,1)S(1)} %pad_maximum_fusion.1.refs_5_), channel_id=1, source_target_pairs={{0,1},{1,0},{2,3},{3,2},{4,5},{5,4},{6,7},{7,6},{8,9},{9,8},{10,11... | collective-permute-start | bytes 688136 | tf_op jit(solution)/shard_map/ppermute | solution.py:216
  53.5 3.2 %collective-permute-done.15.refs_8_ = bf16[4,224,128]{2,1,0:T(8,128)(2,1)S(1)} collective-permute-done((bf16[4,224,128]{2,1,0:T(8,128)(2,1)S(1)}, bf16[4,224,128]{2,1,0:T(8,128)(2,1)S(1)}, u32[]{:S(2)}, u32[]{:S(2)}) %collective-permute-start.15) | collective-permute-done | bytes 229408 | tf_op jit(solution)/shard_map/ppermute | solution.py:216
  56.7 2.7 %collective-permute-start.19 = (bf16[4,224,128]{2,1,0:T(8,128)(2,1)S(1)}, bf16[4,224,128]{2,1,0:T(8,128)(2,1)S(1)}, u32[]{:S(2)}, u32[]{:S(2)}) collective-permute-start(bf16[4,224,128]{2,1,0:T(8,128)(2,1)S(1)} %collective-permute-done.15.refs_8_), channel_id=1, source_target_pairs={{0,1},{1,0},{2,3},{3,2},{4,5},{5,4},{6,7},{7,6},{8,9},{9,8},{10,11... | collective-permute-start | bytes 688136 | tf_op jit(solution)/shard_map/ppermute | solution.py:216
  59.5 3.2 %collective-permute-done.14.refs_7_ = bf16[4,224,128]{2,1,0:T(8,128)(2,1)S(1)} collective-permute-done((bf16[4,224,128]{2,1,0:T(8,128)(2,1)S(1)}, bf16[4,224,128]{2,1,0:T(8,128)(2,1)S(1)}, u32[]{:S(2)}, u32[]{:S(2)}) %collective-permute-start.14) | collective-permute-done | bytes 229408 | tf_op jit(solution)/shard_map/ppermute | solution.py:216
  62.7 0.5 collective-permute-start.18
  63.2 0.3 collective-permute-start.17
  63.5 0.8 collective-permute-done.18.refs_11_
  64.3 0.4 collective-permute-done.17.refs_10_
  64.7 14.8 %denoise.1 = f32[32,128]{1,0:T(8,128)S(1)} custom-call(s32[8]{0:T(128)S(1)} %copy-done.6, f32[64,512]{1,0:T(8,128)S(1)} %bitcast.29, f32[4,64,512]{2,1,0:T(8,128)S(1)} %bitcast.26, bf16[8,80,192]{2,1,0:T(8,128)(2,1)S(1)} %get-tuple-element.13.refs_3_, bf16[1536,128]{1,0:T(8,128)(2,1)S(1)} %get-tuple-element.14.refs_1_.refs_4_, ...), custom_call_target="tpu_custom_call" | custom-call | tf_op jit(solution)/shard_map/denoise/pallas_call | solution.py:740
  79.5 1.5 %collective-permute-start.22 = (f32[32,128]{1,0:T(8,128)S(1)}, f32[32,128]{1,0:T(8,128)S(1)}, u32[]{:S(2)}, u32[]{:S(2)}) collective-permute-start(f32[32,128]{1,0:T(8,128)S(1)} %denoise.1), channel_id=1, source_target_pairs={{0,6},{1,7},{2,4},{3,5},{4,2},{5,3},{6,0},{7,1},{8,14},{9,15},{10,... | collective-permute-start | bytes 49160 | tf_op jit(solution)/shard_map/ppermute | solution.py:216
  81.0 2.1 %collective-permute-start.20 = (f32[32,128]{1,0:T(8,128)S(1)}, f32[32,128]{1,0:T(8,128)S(1)}, u32[]{:S(2)}, u32[]{:S(2)}) collective-permute-start(f32[32,128]{1,0:T(8,128)S(1)} %denoise.1), channel_id=1, source_target_pairs={{0,2},{1,3},{2,0},{3,1},{4,6},{5,7},{6,4},{7,5},{8,10},{9,11},{10,... | collective-permute-start | bytes 49160 | tf_op jit(solution)/shard_map/ppermute | solution.py:216
  83.1 0.8 collective-permute-done.22
  83.9 0.9 collective-permute-done.21
  84.8 1.4 %collective-permute-start.25 = (f32[4,32,128]{2,1,0:T(8,128)S(1)}, f32[4,32,128]{2,1,0:T(8,128)S(1)}, u32[]{:S(2)}, u32[]{:S(2)}) collective-permute-start(f32[4,32,128]{2,1,0:T(8,128)S(1)} %pad_maximum_fusion.3), channel_id=1, source_target_pairs={{0,24},{8,16},{16,8},{24,0},{1,25},{9,17},{17,9},{25,1},{2,26},{10... | collective-permute-start | bytes 196616 | tf_op jit(solution)/shard_map/ppermute | solution.py:216
  86.3 1.2 %collective-permute-start.23 = (f32[4,32,128]{2,1,0:T(8,128)S(1)}, f32[4,32,128]{2,1,0:T(8,128)S(1)}, u32[]{:S(2)}, u32[]{:S(2)}) collective-permute-start(f32[4,32,128]{2,1,0:T(8,128)S(1)} %pad_maximum_fusion.3), channel_id=1, source_target_pairs={{0,8},{8,0},{16,24},{24,16},{1,9},{9,1},{17,25},{25,17},{2,10},{10... | collective-permute-start | bytes 196616 | tf_op jit(solution)/shard_map/ppermute | solution.py:216
  87.5 1.9 %collective-permute-done.23 = f32[4,32,128]{2,1,0:T(8,128)S(1)} collective-permute-done((f32[4,32,128]{2,1,0:T(8,128)S(1)}, f32[4,32,128]{2,1,0:T(8,128)S(1)}, u32[]{:S(2)}, u32[]{:S(2)}) %collective-permute-start.23) | collective-permute-done | bytes 65568 | tf_op jit(solution)/shard_map/ppermute | solution.py:216
  89.4 0.2 collective-permute-done.24
  89.6 3.1 %collective-permute-start.26 = (f32[16,32,128]{2,1,0:T(8,128)S(1)}, f32[16,32,128]{2,1,0:T(8,128)S(1)}, u32[]{:S(2)}, u32[]{:S(2)}) collective-permute-start(f32[16,32,128]{2,1,0:T(8,128)S(1)} %constant_dynamic-update-slice_fusion.refs_1_), channel_id=1, source_target_pairs={{0,1},{1,0},{2,3},{3,2},{4,5},{5,4},{6,7},{7,6},{8,9},{9,8},{10,11... | collective-permute-start | bytes 786440 | tf_op jit(solution)/shard_map/ppermute | solution.py:216
  92.7 1.2 %collective-permute-done.26.refs_2_ = f32[16,32,128]{2,1,0:T(8,128)S(1)} collective-permute-done((f32[16,32,128]{2,1,0:T(8,128)S(1)}, f32[16,32,128]{2,1,0:T(8,128)S(1)}, u32[]{:S(2)}, u32[]{:S(2)}) %collective-permute-start.26) | collective-permute-done | bytes 262176 | tf_op jit(solution)/shard_map/ppermute | solution.py:216
  93.8 9.5 %decode.1 = (f32[64,512]{1,0:T(8,128)}, bf16[16,2,16,512]{3,2,1,0:T(8,128)(2,1)}) custom-call(s32[32]{0:T(128)S(1)} %copy-done.7, f32[16,32,128]{2,1,0:T(8,128)S(1)} %constant_dynamic-update-slice_fusion.refs_1_, f32[16,32,128]{2,1,0:T(8,128)S(1)} %collective-permute-done.26.refs_2_, bf16[3,3,16,512]{3,2,1,0:T(8,128)(2,1)S(1)} %copy-done.3, ...), custom_call_target="tpu_custom_call" | custom-call | tf_op jit(solution)/shard_map/decode/pallas_call | solution.py:765
  (38 shorter events, 0.4 us)
Async XLA Ops:
  0.6 64.0 %copy-start.6 = (s32[8]{0:T(128)S(1)}, s32[8]{0:T(128)}, u32[]{:S(2)}) copy-start(s32[8]{0:T(128)} %refs_0_.4) | copy-start | bytes 100
  0.6 64.0 %copy-start.1 = (f32[4,512,64]{1,2,0:T(8,128)S(1)}, f32[4,512,64]{1,2,0:T(8,128)}, u32[]{:S(2)}) copy-start(f32[4,512,64]{1,2,0:T(8,128)} %param.15) | copy-start | bytes 1572868
  0.7 64.0 %copy-start.4 = (f32[512,64]{0,1:T(8,128)S(1)}, f32[512,64]{0,1:T(8,128)}, u32[]{:S(2)}) copy-start(f32[512,64]{0,1:T(8,128)} %param.14) | copy-start | bytes 393220
  0.7 93.2 %copy-start.3 = (bf16[3,3,16,512]{3,2,1,0:T(8,128)(2,1)S(1)}, bf16[3,3,16,512]{3,2,1,0:T(8,128)(2,1)}, u32[]{:S(2)}) copy-start(bf16[3,3,16,512]{3,2,1,0:T(8,128)(2,1)} %refs_3_.3) | copy-start | bytes 442372
  0.7 93.2 %copy-start.5 = (f32[512]{0:T(512)S(1)}, f32[512]{0:T(512)}, u32[]{:S(2)}) copy-start(f32[512]{0:T(512)} %param.26) | copy-start | bytes 6148
  0.7 93.2 %copy-start.7 = (s32[32]{0:T(128)S(1)}, s32[32]{0:T(128)}, u32[]{:S(2)}) copy-start(s32[32]{0:T(128)} %refs_0_.5) | copy-start | bytes 388
  3.7 90.2 %copy-start = (bf16[3,3,512,512]{3,2,1,0:T(8,128)(2,1)S(1)}, bf16[3,3,512,512]{3,2,1,0:T(8,128)(2,1)}, u32[]{:S(2)}) copy-start(bf16[3,3,512,512]{3,2,1,0:T(8,128)(2,1)} %refs_5_.3) | copy-start | bytes 14155780
  3.7 4.4 %collective-permute-start.2 = (bf16[48,192]{1,0:T(8,128)(2,1)}, bf16[48,192]{1,0:T(8,128)(2,1)S(1)}, u32[]{:S(2)}, u32[]{:S(2)}) collective-permute-start(bf16[48,192]{1,0:T(8,128)(2,1)} %get-tuple-element.12), channel_id=1, source_target_pairs={{0,24},{8,16},{16,8},{24,0},{1,25},{9,17},{17,9},{25,1},{2,26},{10... | collective-permute-start | bytes 55304 | tf_op jit(solution)/shard_map/ppermute | solution.py:216
  6.7 2.9 %collective-permute-start.1 = (bf16[48,192]{1,0:T(8,128)(2,1)}, bf16[48,192]{1,0:T(8,128)(2,1)S(1)}, u32[]{:S(2)}, u32[]{:S(2)}) collective-permute-start(bf16[48,192]{1,0:T(8,128)(2,1)} %get-tuple-element.12), channel_id=1, source_target_pairs={{0,16},{8,24},{16,0},{24,8},{1,17},{9,25},{17,1},{25,9},{2,18},{10... | collective-permute-start | bytes 55304 | tf_op jit(solution)/shard_map/ppermute | solution.py:216
  6.9 2.9 %collective-permute-start = (bf16[48,192]{1,0:T(8,128)(2,1)}, bf16[48,192]{1,0:T(8,128)(2,1)S(1)}, u32[]{:S(2)}, u32[]{:S(2)}) collective-permute-start(bf16[48,192]{1,0:T(8,128)(2,1)} %get-tuple-element.12), channel_id=1, source_target_pairs={{0,8},{8,0},{16,24},{24,16},{1,9},{9,1},{17,25},{25,17},{2,10},{10... | collective-permute-start | bytes 55304 | tf_op jit(solution)/shard_map/ppermute | solution.py:216
  10.5 4.4 %collective-permute-start.4 = (bf16[4,48,192]{2,1,0:T(8,128)(2,1)S(1)}, bf16[4,48,192]{2,1,0:T(8,128)(2,1)S(1)}, u32[]{:S(2)}, u32[]{:S(2)}) collective-permute-start(bf16[4,48,192]{2,1,0:T(8,128)(2,1)S(1)} %get-tuple-element.23), channel_id=1, source_target_pairs={{0,4},{1,5},{2,6},{3,7},{4,0},{5,1},{6,2},{7,3},{8,12},{9,13},{10,... | collective-permute-start | bytes 221192 | tf_op jit(solution)/shard_map/ppermute | solution.py:216
  12.9 3.5 %collective-permute-start.3 = (bf16[4,48,192]{2,1,0:T(8,128)(2,1)S(1)}, bf16[4,48,192]{2,1,0:T(8,128)(2,1)S(1)}, u32[]{:S(2)}, u32[]{:S(2)}) collective-permute-start(bf16[4,48,192]{2,1,0:T(8,128)(2,1)S(1)} %get-tuple-element.23), channel_id=1, source_target_pairs={{0,2},{1,3},{2,0},{3,1},{4,6},{5,7},{6,4},{7,5},{8,10},{9,11},{10,... | collective-permute-start | bytes 221192 | tf_op jit(solution)/shard_map/ppermute | solution.py:216
  14.2 6.4 %collective-permute-start.5 = (bf16[4,48,192]{2,1,0:T(8,128)(2,1)S(1)}, bf16[4,48,192]{2,1,0:T(8,128)(2,1)S(1)}, u32[]{:S(2)}, u32[]{:S(2)}) collective-permute-start(bf16[4,48,192]{2,1,0:T(8,128)(2,1)S(1)} %get-tuple-element.23), channel_id=1, source_target_pairs={{0,6},{1,7},{2,4},{3,5},{4,2},{5,3},{6,0},{7,1},{8,14},{9,15},{10,... | collective-permute-start | bytes 221192 | tf_op jit(solution)/shard_map/ppermute | solution.py:216
  14.2 12.2 %collective-permute-start.7 = (bf16[1152,128]{1,0:T(8,128)(2,1)}, bf16[1152,128]{1,0:T(8,128)(2,1)S(1)}, u32[]{:S(2)}, u32[]{:S(2)}) collective-permute-start(bf16[1152,128]{1,0:T(8,128)(2,1)} %get-tuple-element.17), channel_id=1, source_target_pairs={{0,8},{8,0},{16,24},{24,16},{1,9},{9,1},{17,25},{25,17},{2,10},{10... | collective-permute-start | bytes 884744 | tf_op jit(solution)/shard_map/ppermute | solution.py:216
  20.7 4.5 %collective-permute-start.6 = (bf16[4,4,48,192]{3,2,1,0:T(8,128)(2,1)S(1)}, bf16[4,4,48,192]{3,2,1,0:T(8,128)(2,1)S(1)}, u32[]{:S(2)}, u32[]{:S(2)}) collective-permute-start(bf16[4,4,48,192]{3,2,1,0:T(8,128)(2,1)S(1)} %pad_maximum_fusion.refs_0_), channel_id=1, source_target_pairs={{0,1},{1,0},{2,3},{3,2},{4,5},{5,4},{6,7},{7,6},{8,9},{9,8},{10,11... | collective-permute-start | bytes 884744 | tf_op jit(solution)/shard_map/ppermute | solution.py:216
  23.7 15.0 %collective-permute-start.8 = (bf16[1152,128]{1,0:T(8,128)(2,1)}, bf16[1152,128]{1,0:T(8,128)(2,1)S(1)}, u32[]{:S(2)}, u32[]{:S(2)}) collective-permute-start(bf16[1152,128]{1,0:T(8,128)(2,1)} %get-tuple-element.18), channel_id=1, source_target_pairs={{0,16},{8,24},{16,0},{24,8},{1,17},{9,25},{17,1},{25,9},{2,18},{10... | collective-permute-start | bytes 884744 | tf_op jit(solution)/shard_map/ppermute | solution.py:216
  25.1 13.7 %collective-permute-start.9 = (bf16[1152,128]{1,0:T(8,128)(2,1)}, bf16[1152,128]{1,0:T(8,128)(2,1)S(1)}, u32[]{:S(2)}, u32[]{:S(2)}) collective-permute-start(bf16[1152,128]{1,0:T(8,128)(2,1)} %get-tuple-element.19), channel_id=1, source_target_pairs={{0,24},{8,16},{16,8},{24,0},{1,25},{9,17},{17,9},{25,1},{2,26},{10... | collective-permute-start | bytes 884744 | tf_op jit(solution)/shard_map/ppermute | solution.py:216
  38.8 1.0 copy-start.2
  41.0 5.0 %collective-permute-start.12 = (bf16[224,128]{1,0:T(8,128)(2,1)S(1)}, bf16[224,128]{1,0:T(8,128)(2,1)S(1)}, u32[]{:S(2)}, u32[]{:S(2)}) collective-permute-start(bf16[224,128]{1,0:T(8,128)(2,1)S(1)} %combine_weights.1), channel_id=1, source_target_pairs={{0,6},{1,7},{2,4},{3,5},{4,2},{5,3},{6,0},{7,1},{8,14},{9,15},{10,... | collective-permute-start | bytes 172040 | tf_op jit(solution)/shard_map/ppermute | solution.py:216
  42.8 6.4 %collective-permute-start.11 = (bf16[224,128]{1,0:T(8,128)(2,1)S(1)}, bf16[224,128]{1,0:T(8,128)(2,1)S(1)}, u32[]{:S(2)}, u32[]{:S(2)}) collective-permute-start(bf16[224,128]{1,0:T(8,128)(2,1)S(1)} %combine_weights.1), channel_id=1, source_target_pairs={{0,4},{1,5},{2,6},{3,7},{4,0},{5,1},{6,2},{7,3},{8,12},{9,13},{10,... | collective-permute-start | bytes 172040 | tf_op jit(solution)/shard_map/ppermute | solution.py:216
  43.0 6.2 %collective-permute-start.10 = (bf16[224,128]{1,0:T(8,128)(2,1)S(1)}, bf16[224,128]{1,0:T(8,128)(2,1)S(1)}, u32[]{:S(2)}, u32[]{:S(2)}) collective-permute-start(bf16[224,128]{1,0:T(8,128)(2,1)S(1)} %combine_weights.1), channel_id=1, source_target_pairs={{0,2},{1,3},{2,0},{3,1},{4,6},{5,7},{6,4},{7,5},{8,10},{9,11},{10,... | collective-permute-start | bytes 172040 | tf_op jit(solution)/shard_map/ppermute | solution.py:216
  49.3 7.5 %collective-permute-start.15 = (bf16[4,224,128]{2,1,0:T(8,128)(2,1)S(1)}, bf16[4,224,128]{2,1,0:T(8,128)(2,1)S(1)}, u32[]{:S(2)}, u32[]{:S(2)}) collective-permute-start(bf16[4,224,128]{2,1,0:T(8,128)(2,1)S(1)} %pad_maximum_fusion.1.refs_5_), channel_id=1, source_target_pairs={{0,24},{8,16},{16,8},{24,0},{1,25},{9,17},{17,9},{25,1},{2,26},{10... | collective-permute-start | bytes 688136 | tf_op jit(solution)/shard_map/ppermute | solution.py:216
  50.8 11.9 %collective-permute-start.14 = (bf16[4,224,128]{2,1,0:T(8,128)(2,1)S(1)}, bf16[4,224,128]{2,1,0:T(8,128)(2,1)S(1)}, u32[]{:S(2)}, u32[]{:S(2)}) collective-permute-start(bf16[4,224,128]{2,1,0:T(8,128)(2,1)S(1)} %pad_maximum_fusion.1.refs_5_), channel_id=1, source_target_pairs={{0,16},{8,24},{16,0},{24,8},{1,17},{9,25},{17,1},{25,9},{2,18},{10... | collective-permute-start | bytes 688136 | tf_op jit(solution)/shard_map/ppermute | solution.py:216
  50.9 12.3 %collective-permute-start.13 = (bf16[4,224,128]{2,1,0:T(8,128)(2,1)S(1)}, bf16[4,224,128]{2,1,0:T(8,128)(2,1)S(1)}, u32[]{:S(2)}, u32[]{:S(2)}) collective-permute-start(bf16[4,224,128]{2,1,0:T(8,128)(2,1)S(1)} %pad_maximum_fusion.1.refs_5_), channel_id=1, source_target_pairs={{0,8},{8,0},{16,24},{24,16},{1,9},{9,1},{17,25},{25,17},{2,10},{10... | collective-permute-start | bytes 688136 | tf_op jit(solution)/shard_map/ppermute | solution.py:216
  52.0 11.5 %collective-permute-start.16 = (bf16[4,224,128]{2,1,0:T(8,128)(2,1)S(1)}, bf16[4,224,128]{2,1,0:T(8,128)(2,1)S(1)}, u32[]{:S(2)}, u32[]{:S(2)}) collective-permute-start(bf16[4,224,128]{2,1,0:T(8,128)(2,1)S(1)} %pad_maximum_fusion.1.refs_5_), channel_id=1, source_target_pairs={{0,1},{1,0},{2,3},{3,2},{4,5},{5,4},{6,7},{7,6},{8,9},{9,8},{10,11... | collective-permute-start | bytes 688136 | tf_op jit(solution)/shard_map/ppermute | solution.py:216
  56.7 6.8 %collective-permute-start.19 = (bf16[4,224,128]{2,1,0:T(8,128)(2,1)S(1)}, bf16[4,224,128]{2,1,0:T(8,128)(2,1)S(1)}, u32[]{:S(2)}, u32[]{:S(2)}) collective-permute-start(bf16[4,224,128]{2,1,0:T(8,128)(2,1)S(1)} %collective-permute-done.15.refs_8_), channel_id=1, source_target_pairs={{0,1},{1,0},{2,3},{3,2},{4,5},{5,4},{6,7},{7,6},{8,9},{9,8},{10,11... | collective-permute-start | bytes 688136 | tf_op jit(solution)/shard_map/ppermute | solution.py:216
  62.7 1.6 %collective-permute-start.18 = (bf16[4,224,128]{2,1,0:T(8,128)(2,1)S(1)}, bf16[4,224,128]{2,1,0:T(8,128)(2,1)S(1)}, u32[]{:S(2)}, u32[]{:S(2)}) collective-permute-start(bf16[4,224,128]{2,1,0:T(8,128)(2,1)S(1)} %collective-permute-done.14.refs_7_), channel_id=1, source_target_pairs={{0,1},{1,0},{2,3},{3,2},{4,5},{5,4},{6,7},{7,6},{8,9},{9,8},{10,11... | collective-permute-start | bytes 688136 | tf_op jit(solution)/shard_map/ppermute | solution.py:216
  63.2 1.5 %collective-permute-start.17 = (bf16[4,224,128]{2,1,0:T(8,128)(2,1)S(1)}, bf16[4,224,128]{2,1,0:T(8,128)(2,1)S(1)}, u32[]{:S(2)}, u32[]{:S(2)}) collective-permute-start(bf16[4,224,128]{2,1,0:T(8,128)(2,1)S(1)} %collective-permute-done.13.refs_6_), channel_id=1, source_target_pairs={{0,1},{1,0},{2,3},{3,2},{4,5},{5,4},{6,7},{7,6},{8,9},{9,8},{10,11... | collective-permute-start | bytes 688136 | tf_op jit(solution)/shard_map/ppermute | solution.py:216
  79.5 4.5 %collective-permute-start.22 = (f32[32,128]{1,0:T(8,128)S(1)}, f32[32,128]{1,0:T(8,128)S(1)}, u32[]{:S(2)}, u32[]{:S(2)}) collective-permute-start(f32[32,128]{1,0:T(8,128)S(1)} %denoise.1), channel_id=1, source_target_pairs={{0,6},{1,7},{2,4},{3,5},{4,2},{5,3},{6,0},{7,1},{8,14},{9,15},{10,... | collective-permute-start | bytes 49160 | tf_op jit(solution)/shard_map/ppermute | solution.py:216
  81.0 3.8 %collective-permute-start.21 = (f32[32,128]{1,0:T(8,128)S(1)}, f32[32,128]{1,0:T(8,128)S(1)}, u32[]{:S(2)}, u32[]{:S(2)}) collective-permute-start(f32[32,128]{1,0:T(8,128)S(1)} %denoise.1), channel_id=1, source_target_pairs={{0,4},{1,5},{2,6},{3,7},{4,0},{5,1},{6,2},{7,3},{8,12},{9,13},{10,... | collective-permute-start | bytes 49160 | tf_op jit(solution)/shard_map/ppermute | solution.py:216
  81.0 3.8 %collective-permute-start.20 = (f32[32,128]{1,0:T(8,128)S(1)}, f32[32,128]{1,0:T(8,128)S(1)}, u32[]{:S(2)}, u32[]{:S(2)}) collective-permute-start(f32[32,128]{1,0:T(8,128)S(1)} %denoise.1), channel_id=1, source_target_pairs={{0,2},{1,3},{2,0},{3,1},{4,6},{5,7},{6,4},{7,5},{8,10},{9,11},{10,... | collective-permute-start | bytes 49160 | tf_op jit(solution)/shard_map/ppermute | solution.py:216
  84.8 4.8 %collective-permute-start.25 = (f32[4,32,128]{2,1,0:T(8,128)S(1)}, f32[4,32,128]{2,1,0:T(8,128)S(1)}, u32[]{:S(2)}, u32[]{:S(2)}) collective-permute-start(f32[4,32,128]{2,1,0:T(8,128)S(1)} %pad_maximum_fusion.3), channel_id=1, source_target_pairs={{0,24},{8,16},{16,8},{24,0},{1,25},{9,17},{17,9},{25,1},{2,26},{10... | collective-permute-start | bytes 196616 | tf_op jit(solution)/shard_map/ppermute | solution.py:216
  86.2 3.4 %collective-permute-start.24 = (f32[4,32,128]{2,1,0:T(8,128)S(1)}, f32[4,32,128]{2,1,0:T(8,128)S(1)}, u32[]{:S(2)}, u32[]{:S(2)}) collective-permute-start(f32[4,32,128]{2,1,0:T(8,128)S(1)} %pad_maximum_fusion.3), channel_id=1, source_target_pairs={{0,16},{8,24},{16,0},{24,8},{1,17},{9,25},{17,1},{25,9},{2,18},{10... | collective-permute-start | bytes 196616 | tf_op jit(solution)/shard_map/ppermute | solution.py:216
  86.3 3.1 %collective-permute-start.23 = (f32[4,32,128]{2,1,0:T(8,128)S(1)}, f32[4,32,128]{2,1,0:T(8,128)S(1)}, u32[]{:S(2)}, u32[]{:S(2)}) collective-permute-start(f32[4,32,128]{2,1,0:T(8,128)S(1)} %pad_maximum_fusion.3), channel_id=1, source_target_pairs={{0,8},{8,0},{16,24},{24,16},{1,9},{9,1},{17,25},{25,17},{2,10},{10... | collective-permute-start | bytes 196616 | tf_op jit(solution)/shard_map/ppermute | solution.py:216
  89.6 4.2 %collective-permute-start.26 = (f32[16,32,128]{2,1,0:T(8,128)S(1)}, f32[16,32,128]{2,1,0:T(8,128)S(1)}, u32[]{:S(2)}, u32[]{:S(2)}) collective-permute-start(f32[16,32,128]{2,1,0:T(8,128)S(1)} %constant_dynamic-update-slice_fusion.refs_1_), channel_id=1, source_target_pairs={{0,1},{1,0},{2,3},{3,2},{4,5},{5,4},{6,7},{7,6},{8,9},{9,8},{10,11... | collective-permute-start | bytes 786440 | tf_op jit(solution)/shard_map/ppermute | solution.py:216
where the time goes:
time: 104 us; the launch traced here: 103 us
  waiting for transfers between devices  38.3 us (37%)
  starting transfers between devices  32.6 us (31%)
  Pallas kernels  29.7 us (29%)
    ppermute x27, waiting for transfers between devices, xor_pieces(): lax.ppermute(value, axis, [(i, i ^ mask) for i in range(count)])  38.3 us
    ppermute x27, starting transfers between devices, xor_pieces(): lax.ppermute(value, axis, [(i, i ^ mask) for i in range(count)])  32.6 us
    pallas_call x1, Pallas kernels, per_device_fast(): pl.pallas_call(functools.partial(loop_kernel, (features, mp_count, prompt...  14.8 us
    pallas_call x1, Pallas kernels, per_device_fast(): pl.pallas_call(functools.partial(decode_kernel, (segments, mp_count, samp...  9.48 us
    pallas_call x1, Pallas kernels, per_device_fast(): pl.pallas_call(functools.partial(split_kernel, (segments, quarter)), out_...  2.98 us
  transfers between devices with their start and end apart: 27, of which 18 were waited for; matrix products, arithmetic and copies ran while one was open for 0% of the time, Pallas kernels for 1%

commit v1 on v0

--- a/solution.py
+++ b/solution.py
@@ -18,7 +18,8 @@
 LATENT_SCALE = 1.0 / 1.5305
 EPSILON = 1e-06
 GELU_A = math.sqrt(2.0 / math.pi)
-GELU_B = GELU_A * 0.044715
+GELU_S = (GELU_A * 0.044715) ** (1.0 / 3.0)
+GELU_C = GELU_A / GELU_S
 
 
 def with_halo(cells, sides, width):
@@ -315,27 +316,28 @@
         source * in_rows + inner,
         jnp.where(
             inner < 2 * in_rows,
-            192 + source * in_rows + inner - in_rows,
+            128 + source * in_rows + inner - in_rows,
             jnp.where(
                 inner < 2 * in_rows + prompt_rows,
                 64 + source * prompt_rows + inner - 2 * in_rows,
                 jnp.where(
                     (block == 0) & (inner < 2 * in_rows + prompt_rows + 2),
                     64 + prompts + inner - 2 * in_rows - prompt_rows,
-                    1000,
+                    -1,
                 ),
             ),
         ),
     )
     row = lax.broadcasted_iota(jnp.int32, (256, stack), 0)
-    place = (row == target).astype(jnp.float32).astype(jnp.bfloat16)
+    again = (target >= 128) & (row == target + 64)
+    place = ((row == target) | again).astype(jnp.float32).astype(jnp.bfloat16)
     total = jnp.zeros((128, 1), jnp.float32)
     for index in range(slices):
         ref = own if index % 2 == 0 else other
         where_to = lax.bitwise_xor(mp, index)
         both = dot32(place, ref[index // 2].reshape(stack, width))
         canon[where_to] = both[0:128]
-        table_ref[where_to] = both[0:80].astype(jnp.bfloat16)
+        table_ref[where_to] = both[0:128].astype(jnp.bfloat16)
         start = pl.multiple_of(where_to * width, width)
         w_out_ref[pl.ds(start, width), :] = jnp.transpose(both[128:256]).astype(jnp.bfloat16)
         total = total + jnp.sum(both[0:128], axis=1, keepdims=True)
@@ -380,39 +382,69 @@
                 blocks[other, at : at + quarter, :], w_out_ref[pl.ds(start, 128), :]
             )
     lane = lax.broadcasted_iota(jnp.int32, (1, 128), 1)
-    down = 0.5 * down
-    piece_ref[0:128, :] = jnp.where(lane < 64, jnp.transpose(main), down[0:128]).astype(
+    down = (0.5 / GELU_S) * down
+    piece_ref[0:80, :] = main[0:80].astype(jnp.bfloat16)
+    beside = pltpu.roll(tail, 64, 1)
+    piece_ref[80:128, :] = jnp.where(lane < 64, tail[0:48], beside[32:80]).astype(jnp.bfloat16)
+    piece_ref[128:192, :] = jnp.where(lane < 64, down[0:64], down[64:128]).astype(jnp.bfloat16)
+    piece_ref[192:224, :] = jnp.where(lane < 64, down[128:160], down[160:192]).astype(
         jnp.bfloat16
     )
-    piece_ref[128:192, :] = jnp.where(
-        lane < 64, jnp.transpose(tail)[0:64], down[128:192]
-    ).astype(jnp.bfloat16)
-    piece_ref[192:208, :] = main[64:80].astype(jnp.bfloat16)
-    piece_ref[208:224, :] = tail[64:80].astype(jnp.bfloat16)
+
+
+def moment_kernel(features, table_ref, w_out_ref, moment_ref):
+    slices, rows, width = table_ref.shape
+    total = jnp.zeros((rows, 1), jnp.float32)
+    for index in range(slices):
+        total = total + jnp.sum(table_ref[index].astype(jnp.float32), axis=1, keepdims=True)
+    average = total / features
+    gram = jnp.zeros((rows, rows), jnp.float32)
+    velocity = jnp.zeros((rows, 128), jnp.float32)
+    for index in range(slices):
+        raw = table_ref[index]
+        centered = raw.astype(jnp.float32) - average
+        gram = gram + lax.dot_general(
+            centered,
+            centered,
+            (((1,), (1,)), ((), ())),
+            precision=lax.Precision.HIGHEST,
+            preferred_element_type=jnp.float32,
+        )
+        velocity = velocity + dot32(raw, w_out_ref[index * width : (index + 1) * width, :])
+    for index, part in enumerate(split_three(gram) + split_three(velocity)[:2]):
+        moment_ref[:, index * 128 : (index + 1) * 128] = part
 
 
 def loop_kernel(cfg, *refs):
-    features, slices, prompts, chunk = cfg
-    assign_ref, noise_ref, step_ref, table_ref, w_out_ref = refs[:5]
-    pieces = refs[5:-9]
-    result_ref, state, steps, const, hidden, weights, extras, turned, sems = refs[-9:]
+    features, prompts = cfg
+    assign_ref, noise_ref, step_ref, moment_ref = refs[:4]
+    pieces = refs[4:-9]
+    result_ref, state, steps, first, second, narrow, packed, turned, sems = refs[-9:]
     mp = lax.axis_index("mp")
     tokens = state.shape[0]
-    width = table_ref.shape[2]
     pair = lax.shift_right_logical(mp, 1)
     odd = lax.bitwise_and(mp, 1)
+    lines = narrow.shape[1]
     copies = []
     for i, ref in enumerate(pieces):
+        for j in range(lines):
+            at = i * 768 + (384 * (j % 2) + 128 * (j // 2))
+            copies.append(
+                pltpu.make_async_copy(
+                    ref.at[j, 0:80, :], first.at[:, at : at + 128], sems.at[i, j]
+                )
+            )
         copies.append(
-            pltpu.make_async_copy(ref.at[:, 0:192, :], weights.at[i], sems.at[2 * i])
+            pltpu.make_async_copy(ref.at[:, 80:128, :], narrow.at[i], sems.at[i, lines])
         )
         copies.append(
-            pltpu.make_async_copy(ref.at[:, 192:224, :], extras.at[i], sems.at[2 * i + 1])
+            pltpu.make_async_copy(ref.at[:, 128:224, :], packed.at[i], sems.at[i, lines + 1])
         )
     for copy in copies:
         copy.start()
     prompt = assign_ref[mp]
     lane = lax.broadcasted_iota(jnp.int32, (1, 128), 1)
+    low = lane < 64
     lanes_from = pl.multiple_of(pair * 128, 128)
     rows_from = pl.multiple_of(odd * tokens, tokens)
     steps[...] = jnp.zeros_like(steps)
@@ -422,75 +454,53 @@
     for index in range(STEPS):
         turned[...] = jnp.transpose(step_ref[index, :, pl.ds(lanes_from, 128)])
         steps[index, :, 0:64] = turned[pl.ds(rows_from, tokens), :]
-    sixteen = lax.broadcasted_iota(jnp.int32, (16, 1), 0)
-    pick = (sixteen == prompt).astype(jnp.float32)
-    timing = (sixteen == prompts).astype(jnp.float32)
+    pick = (lane == 64 + prompt).astype(jnp.float32)
+    timing = (lane == 64 + prompts).astype(jnp.float32)
     for copy in copies:
         copy.wait()
-    flat = [(i, j) for i in range(len(pieces)) for j in range(weights.shape[1])]
-    for two in range(len(flat) // 2):
-        e = [
-            extras[flat[two * 2 + h][0], flat[two * 2 + h][1], 16 * i : 16 * i + 16, :].astype(
-                jnp.float32
-            )
-            for h in range(2)
-            for i in range(2)
-        ]
-        moved = pltpu.roll(e[2], 64, 1)
-        lanes = [
-            e[0],
-            jnp.where(lane < 64, e[1], moved),
-            jnp.where(lane < 64, moved, pltpu.roll(e[3], 64, 1)),
-        ]
-        for third in range(3):
-            at = two * 384 + third * 128
-            const[0:1, at : at + 128] = jnp.sum(pick * lanes[third], axis=0, keepdims=True)
-            const[1:2, at : at + 128] = jnp.sum(timing * lanes[third], axis=0, keepdims=True)
-    count = len(flat) * 192
+
+    def swap(value):
+        return pltpu.roll(value.astype(jnp.float32), 64, 1).astype(jnp.bfloat16)
+
+    for i in range(len(pieces)):
+        for two in range(lines // 2):
+            left, right = narrow[i, 2 * two], narrow[i, 2 * two + 1]
+            at = i * 768 + 384 * two + 256
+            first[0:48, at : at + 128] = jnp.where(low, left, swap(right))
+            first[48:80, at : at + 128] = jnp.where(low, swap(left)[16:48], right[16:48])
+            left, right = packed[i, 2 * two], packed[i, 2 * two + 1]
+            at = i * 384 + 128 * two
+            second[at : at + 64, :] = jnp.where(low, left[0:64], swap(right[0:64]))
+            second[at + 64 : at + 128, :] = jnp.where(low, swap(left[0:64]), right[0:64])
+            left, right = packed[i, two, 64:96], packed[i, two + 2, 64:96]
+            at = i * 384 + 256 + 64 * two
+            second[at : at + 32, :] = jnp.where(low, left, swap(right))
+            second[at + 32 : at + 64, :] = jnp.where(low, swap(left), right)
     step_size = 1.0 / STEPS
     noise_gain = NOISE_SCALE * math.sqrt(step_size)
 
     def one_step(step, carry):
         time_now = 1.0 - step.astype(jnp.float32) * step_size
         now = state[...]
-        operand = now.astype(jnp.bfloat16)
-        narrow = operand[:, 0:64]
-        weight = pick + time_now * timing
-        total = jnp.zeros((tokens, 1), jnp.float32)
-        for index in range(slices):
-            base = jnp.sum(
-                table_ref[index, 64:80, :].astype(jnp.float32) * weight, axis=0, keepdims=True
+        full = (now + pick + time_now * timing).astype(jnp.bfloat16)
+        moments = dot32(full, moment_ref[...])
+        quadratic = moments[:, 0:128] + moments[:, 128:256] + moments[:, 256:384]
+        square = jnp.sum(full.astype(jnp.float32) * quadratic, axis=1, keepdims=True)
+        scale = GELU_S * lax.rsqrt(jnp.maximum(square / features, 0.0) + EPSILON)
+        total = jnp.zeros((2 * tokens, 128), jnp.float32)
+        for i in range(len(pieces)):
+            acts = []
+            for at in (i * 768, i * 768 + 384):
+                pre = dot32(full[:, 0:80], first[:, at : at + 384]) * scale
+                inner = pre * (GELU_C + pre * pre)
+                acts.append((pre + pre * jnp.tanh(inner)).astype(jnp.bfloat16))
+            total = total + dot32(
+                jnp.concatenate(acts, axis=0), second[i * 384 : (i + 1) * 384, :]
             )
-            value = dot32(narrow, table_ref[index, 0:64, :]) + base
-            hidden[index] = value
-            total = total + jnp.sum(value, axis=1, keepdims=True)
-        average = total / features
-        square = jnp.zeros((tokens, 1), jnp.float32)
-        velocity = jnp.zeros((tokens, 128), jnp.float32)
-        for index in range(slices):
-            value = hidden[index]
-            centered = value - average
-            square = square + jnp.sum(centered * centered, axis=1, keepdims=True)
-            velocity = velocity + dot32(
-                value.astype(jnp.bfloat16), w_out_ref[index * width : (index + 1) * width, :]
-            )
-        spread = lax.rsqrt(square / features + EPSILON)
-        per_block = weights.shape[1] * 192
-        for at in range(0, count, chunk):
-            block = at // per_block
-            inside = (at % per_block) // 192
-            part = weights[block, inside : inside + chunk // 192].reshape(chunk, 128)
-            shift = const[0:1, at : at + chunk] + time_now * const[1:2, at : at + chunk]
-            pre = lax.dot_general(
-                operand, part, (((1,), (1,)), ((), ())), preferred_element_type=jnp.float32
-            )
-            pre = (pre + shift) * spread
-            inner = pre * (GELU_A + GELU_B * (pre * pre))
-            act = (pre + pre * jnp.tanh(inner)).astype(jnp.bfloat16)
-            velocity = velocity + dot32(act, part)
-        moved = pltpu.roll(velocity, 64, 1)
-        fresh = now - step_size * moved + noise_gain * steps[step]
-        state[...] = jnp.where(lane < 64, fresh, 0.0)
+        velocity = moments[:, 384:512] + moments[:, 512:640]
+        velocity = velocity + total[0:tokens] + pltpu.roll(total[tokens : 2 * tokens], 64, 1)
+        fresh = now - step_size * velocity + noise_gain * steps[step]
+        state[...] = jnp.where(low, fresh, 0.0)
         return carry
 
     lax.fori_loop(0, STEPS, one_step, 0)
@@ -705,7 +715,7 @@
         functools.partial(table_kernel, (segments, features, mp_count, latent, prompts)),
         out_shape=[
             jax.ShapeDtypeStruct((mp_count, 256, width), bf16),
-            jax.ShapeDtypeStruct((mp_count, 80, width), bf16),
+            jax.ShapeDtypeStruct((mp_count, 128, width), bf16),
             jax.ShapeDtypeStruct((features, 128), bf16),
         ],
         in_specs=[any_space] * 2,
@@ -737,24 +747,32 @@
         plane += xor_pieces(line, "segment", [other])
     plane = plane + [xor_pieces(block, "mp", [1])[0] for block in plane]
     half = mp_count // 2
+    moments = pl.pallas_call(
+        functools.partial(moment_kernel, features),
+        out_shape=jax.ShapeDtypeStruct((128, 640), bf16),
+        in_specs=whole(2),
+        out_specs=whole(1)[0],
+        compiler_params=pltpu.CompilerParams(vmem_limit_bytes=8 * MIB),
+        name="moments",
+    )(tables, w_out_all)
     result = pl.pallas_call(
-        functools.partial(loop_kernel, (features, mp_count, prompts, 384)),
+        functools.partial(loop_kernel, (features, prompts)),
         out_shape=jax.ShapeDtypeStruct((tokens // 2, 128), f32),
-        in_specs=[smem] + whole(4) + [any_space] * len(plane),
+        in_specs=[smem] + whole(3) + [any_space] * len(plane),
         out_specs=whole(1)[0],
         scratch_shapes=[
             pltpu.VMEM((tokens, 128), f32),
             pltpu.VMEM((STEPS, tokens, 128), f32),
-            pltpu.VMEM((8, len(plane) * half * quarter), f32),
-            pltpu.VMEM((mp_count, tokens, width), f32),
-            pltpu.VMEM((len(plane), half, quarter, 128), bf16),
-            pltpu.VMEM((len(plane), half, 32, 128), bf16),
+            pltpu.VMEM((80, len(plane) * half * quarter), bf16),
+            pltpu.VMEM((len(plane) * half * quarter // 2, 128), bf16),
+            pltpu.VMEM((len(plane), half, 48, 128), bf16),
+            pltpu.VMEM((len(plane), half, 96, 128), bf16),
             pltpu.VMEM((128, 64), f32),
-            pltpu.SemaphoreType.DMA((2 * len(plane),)),
+            pltpu.SemaphoreType.DMA((len(plane), half + 2)),
         ],
         compiler_params=pltpu.CompilerParams(vmem_limit_bytes=24 * MIB),
         name="denoise",
-    )(assign, noise_init.T, step_noise.transpose(0, 2, 1), tables, w_out_all, *plane)
+    )(assign, noise_init.T, step_noise.transpose(0, 2, 1), moments, *plane)
     image = jnp.stack([result] + xor_pieces(result, "mp", along))
     image = jnp.concatenate([image] + xor_pieces(image, "segment", around), axis=0)
     (image_other,) = xor_pieces(image, "mp", [1])

time: 104 us -> 96.6 us (0.929)
  Pallas kernels: 29.7 us -> 23.7 us
  waiting for transfers between devices: 38.3 us -> 37.1 us
    pallas_call x1 -> x2, Pallas kernels: 14.8 us -> 8.63 us  [the longest x1 7.32 us: per_device_fast(): pl.pallas_call(functools.partial(loop_kernel, (features, prompts)), out_s...]
    ppermute x27, waiting for transfers between devices: 38.3 us -> 37.1 us  [xor_pieces(): lax.ppermute(value, axis, [(i, i ^ mask) for i in range(count)])]
  transfers between devices with their start and end apart: 27 -> 27, of which waited for: 18 -> 16; matrix products, arithmetic and copies ran while one was open for 0% -> 0% of each run, Pallas kernels for 1% -> 3%
where the time goes in v1:
time: 96.6 us; the launch traced here: 96 us
  waiting for transfers between devices  37.1 us (38%)
  starting transfers between devices  32.5 us (34%)
  Pallas kernels  23.7 us (25%)
  local copies, waits for them, and re-layouts  1.03 us (1%)
    ppermute x27, waiting for transfers between devices, xor_pieces(): lax.ppermute(value, axis, [(i, i ^ mask) for i in range(count)])  37.1 us
    ppermute x27, starting transfers between devices, xor_pieces(): lax.ppermute(value, axis, [(i, i ^ mask) for i in range(count)])  32.5 us
    pallas_call x1, Pallas kernels, per_device_fast(): pl.pallas_call(functools.partial(decode_kernel, (segments, mp_count, samp...  9.47 us
    pallas_call x1, Pallas kernels, per_device_fast(): pl.pallas_call(functools.partial(loop_kernel, (features, prompts)), out_s...  7.32 us
    pallas_call x1, Pallas kernels, per_device_fast(): pl.pallas_call(functools.partial(split_kernel, (segments, quarter)), out_...  3.03 us
  transfers between devices with their start and end apart: 27, of which 16 were waited for; matrix products, arithmetic and copies ran while one was open for 0% of the time, Pallas kernels for 3%

profile of v1, /device:TPU:1, one launch (start us, length us, event | category | flops | bytes accessed | tf_op | source)
XLA Modules:
  0.0 96.0 jit_solution(1854017892228349974)
XLA Ops:
  0.7 3.0 %split_weights.1 = (bf16[48,192]{1,0:T(8,128)(2,1)}, bf16[1152,128]{1,0:T(8,128)(2,1)}, bf16[1152,128]{1,0:T(8,128)(2,1)}, bf16[1152,128]{1,0:T(8,128)(2,1)}, bf16[1152,128]{1,0:T(8,128)(2,1)}) custom-call(bf16[16,192]{1,0:T(8,128)(2,1)} %refs_0_.3, bf16[16,192]{1,0:T(8,128)(2,1)} %bitcast.46, bf16[2,192]{1,0:T(2,128)(2,1)} %refs_2_.1, ...), custom_call_target="tpu_custom_call" | custom-call | tf_op jit(solution)/shard_map/split_weights/pallas_call | solution.py:700
  3.7 3.0 %collective-permute-start.2 = (bf16[48,192]{1,0:T(8,128)(2,1)}, bf16[48,192]{1,0:T(8,128)(2,1)S(1)}, u32[]{:S(2)}, u32[]{:S(2)}) collective-permute-start(bf16[48,192]{1,0:T(8,128)(2,1)} %get-tuple-element.12), channel_id=1, source_target_pairs={{0,24},{8,16},{16,8},{24,0},{1,25},{9,17},{17,9},{25,1},{2,26},{10... | collective-permute-start | bytes 55304 | tf_op jit(solution)/shard_map/ppermute | solution.py:217
  6.7 0.2 collective-permute-start.1
  7.0 1.1 %collective-permute-done.2 = bf16[48,192]{1,0:T(8,128)(2,1)S(1)} collective-permute-done((bf16[48,192]{1,0:T(8,128)(2,1)}, bf16[48,192]{1,0:T(8,128)(2,1)S(1)}, u32[]{:S(2)}, u32[]{:S(2)}) %collective-permute-start.2) | collective-permute-done | bytes 18464 | tf_op jit(solution)/shard_map/ppermute | solution.py:217
  8.1 1.5 %collective-permute-done.1 = bf16[48,192]{1,0:T(8,128)(2,1)S(1)} collective-permute-done((bf16[48,192]{1,0:T(8,128)(2,1)}, bf16[48,192]{1,0:T(8,128)(2,1)S(1)}, u32[]{:S(2)}, u32[]{:S(2)}) %collective-permute-start.1) | collective-permute-done | bytes 18464 | tf_op jit(solution)/shard_map/ppermute | solution.py:217
  9.6 0.2 collective-permute-done
  9.8 0.8 fusion
  10.6 2.4 %collective-permute-start.4 = (bf16[4,48,192]{2,1,0:T(8,128)(2,1)S(1)}, bf16[4,48,192]{2,1,0:T(8,128)(2,1)S(1)}, u32[]{:S(2)}, u32[]{:S(2)}) collective-permute-start(bf16[4,48,192]{2,1,0:T(8,128)(2,1)S(1)} %get-tuple-element.23), channel_id=1, source_target_pairs={{0,4},{1,5},{2,6},{3,7},{4,0},{5,1},{6,2},{7,3},{8,12},{9,13},{10,... | collective-permute-start | bytes 221192 | tf_op jit(solution)/shard_map/ppermute | solution.py:217
  13.0 1.3 %collective-permute-start.3 = (bf16[4,48,192]{2,1,0:T(8,128)(2,1)S(1)}, bf16[4,48,192]{2,1,0:T(8,128)(2,1)S(1)}, u32[]{:S(2)}, u32[]{:S(2)}) collective-permute-start(bf16[4,48,192]{2,1,0:T(8,128)(2,1)S(1)} %get-tuple-element.23), channel_id=1, source_target_pairs={{0,2},{1,3},{2,0},{3,1},{4,6},{5,7},{6,4},{7,5},{8,10},{9,11},{10,... | collective-permute-start | bytes 221192 | tf_op jit(solution)/shard_map/ppermute | solution.py:217
  14.3 0.3 collective-permute-start.7
  14.5 0.5 collective-permute-done.4
  15.1 1.4 %collective-permute-done.3 = bf16[4,48,192]{2,1,0:T(8,128)(2,1)S(1)} collective-permute-done((bf16[4,48,192]{2,1,0:T(8,128)(2,1)S(1)}, bf16[4,48,192]{2,1,0:T(8,128)(2,1)S(1)}, u32[]{:S(2)}, u32[]{:S(2)}) %collective-permute-start.3) | collective-permute-done | bytes 73760 | tf_op jit(solution)/shard_map/ppermute | solution.py:217
  16.5 4.2 %collective-permute-done.5 = bf16[4,48,192]{2,1,0:T(8,128)(2,1)S(1)} collective-permute-done((bf16[4,48,192]{2,1,0:T(8,128)(2,1)S(1)}, bf16[4,48,192]{2,1,0:T(8,128)(2,1)S(1)}, u32[]{:S(2)}, u32[]{:S(2)}) %collective-permute-start.5) | collective-permute-done | bytes 73760 | tf_op jit(solution)/shard_map/ppermute | solution.py:217
  20.7 3.1 %collective-permute-start.6 = (bf16[4,4,48,192]{3,2,1,0:T(8,128)(2,1)S(1)}, bf16[4,4,48,192]{3,2,1,0:T(8,128)(2,1)S(1)}, u32[]{:S(2)}, u32[]{:S(2)}) collective-permute-start(bf16[4,4,48,192]{3,2,1,0:T(8,128)(2,1)S(1)} %pad_maximum_fusion.refs_0_), channel_id=1, source_target_pairs={{0,1},{1,0},{2,3},{3,2},{4,5},{5,4},{6,7},{7,6},{8,9},{9,8},{10,11... | collective-permute-start | bytes 884744 | tf_op jit(solution)/shard_map/ppermute | solution.py:217
  23.8 1.3 %collective-permute-start.8 = (bf16[1152,128]{1,0:T(8,128)(2,1)}, bf16[1152,128]{1,0:T(8,128)(2,1)S(1)}, u32[]{:S(2)}, u32[]{:S(2)}) collective-permute-start(bf16[1152,128]{1,0:T(8,128)(2,1)} %get-tuple-element.18), channel_id=1, source_target_pairs={{0,16},{8,24},{16,0},{24,8},{1,17},{9,25},{17,1},{25,9},{2,18},{10... | collective-permute-start | bytes 884744 | tf_op jit(solution)/shard_map/ppermute | solution.py:217
  25.1 0.1 collective-permute-start.9
  25.3 1.3 %order_tables.1 = (bf16[8,256,192]{2,1,0:T(8,128)(2,1)S(1)}, bf16[8,128,192]{2,1,0:T(8,128)(2,1)S(1)}, bf16[1536,128]{1,0:T(8,128)(2,1)S(1)}) custom-call(bf16[4,4,48,192]{3,2,1,0:T(8,128)(2,1)S(1)} %pad_maximum_fusion.refs_0_, bf16[4,4,48,192]{3,2,1,0:T(8,128)(2,1)S(1)} %collective-permute-done.6.refs_1_), custom_call_target="tpu_custom_call" | custom-call | tf_op jit(solution)/shard_map/order_tables/pallas_call | solution.py:714
  26.6 12.3 %collective-permute-done.8.refs_4_ = bf16[1152,128]{1,0:T(8,128)(2,1)S(1)} collective-permute-done((bf16[1152,128]{1,0:T(8,128)(2,1)}, bf16[1152,128]{1,0:T(8,128)(2,1)S(1)}, u32[]{:S(2)}, u32[]{:S(2)}) %collective-permute-start.8) | collective-permute-done | bytes 294944 | tf_op jit(solution)/shard_map/ppermute | solution.py:217
  38.8 1.0 %copy-done.1 = bf16[1152,128]{1,0:T(8,128)(2,1)S(1)} copy-done((bf16[1152,128]{1,0:T(8,128)(2,1)S(1)}, bf16[1152,128]{1,0:T(8,128)(2,1)}, u32[]{:S(2)}) %copy-start.1) | copy-done | bytes 294936
  39.8 1.2 %combine_weights.1 = bf16[224,128]{1,0:T(8,128)(2,1)S(1)} custom-call(bf16[8,256,192]{2,1,0:T(8,128)(2,1)S(1)} %get-tuple-element.15.refs_0_, bf16[1536,128]{1,0:T(8,128)(2,1)S(1)} %get-tuple-element.14.w_out_ref.refs_1_, bf16[1152,128]{1,0:T(8,128)(2,1)S(1)} %copy-done.1, bf16[1152,128]{1,0:T(8,128)(2,1)S(1)} %collective-permute-done.7.refs_3_, ...), custom_call_target="tpu_custom_call" | custom-call | tf_op jit(solution)/shard_map/combine_weights/pallas_call | solution.py:732
  41.0 1.8 %collective-permute-start.12 = (bf16[224,128]{1,0:T(8,128)(2,1)S(1)}, bf16[224,128]{1,0:T(8,128)(2,1)S(1)}, u32[]{:S(2)}, u32[]{:S(2)}) collective-permute-start(bf16[224,128]{1,0:T(8,128)(2,1)S(1)} %combine_weights.1), channel_id=1, source_target_pairs={{0,6},{1,7},{2,4},{3,5},{4,2},{5,3},{6,0},{7,1},{8,14},{9,15},{10,... | collective-permute-start | bytes 172040 | tf_op jit(solution)/shard_map/ppermute | solution.py:217
  42.9 0.2 collective-permute-start.11
  43.1 1.6 %collective-permute-start.10 = (bf16[224,128]{1,0:T(8,128)(2,1)S(1)}, bf16[224,128]{1,0:T(8,128)(2,1)S(1)}, u32[]{:S(2)}, u32[]{:S(2)}) collective-permute-start(bf16[224,128]{1,0:T(8,128)(2,1)S(1)} %combine_weights.1), channel_id=1, source_target_pairs={{0,2},{1,3},{2,0},{3,1},{4,6},{5,7},{6,4},{7,5},{8,10},{9,11},{10,... | collective-permute-start | bytes 172040 | tf_op jit(solution)/shard_map/ppermute | solution.py:217
  44.7 1.4 %collective-permute-done.12 = bf16[224,128]{1,0:T(8,128)(2,1)S(1)} collective-permute-done((bf16[224,128]{1,0:T(8,128)(2,1)S(1)}, bf16[224,128]{1,0:T(8,128)(2,1)S(1)}, u32[]{:S(2)}, u32[]{:S(2)}) %collective-permute-start.12) | collective-permute-done | bytes 57376 | tf_op jit(solution)/shard_map/ppermute | solution.py:217
  46.1 3.2 %collective-permute-done.11 = bf16[224,128]{1,0:T(8,128)(2,1)S(1)} collective-permute-done((bf16[224,128]{1,0:T(8,128)(2,1)S(1)}, bf16[224,128]{1,0:T(8,128)(2,1)S(1)}, u32[]{:S(2)}, u32[]{:S(2)}) %collective-permute-start.11) | collective-permute-done | bytes 57376 | tf_op jit(solution)/shard_map/ppermute | solution.py:217
  49.3 1.5 %collective-permute-start.15 = (bf16[4,224,128]{2,1,0:T(8,128)(2,1)S(1)}, bf16[4,224,128]{2,1,0:T(8,128)(2,1)S(1)}, u32[]{:S(2)}, u32[]{:S(2)}) collective-permute-start(bf16[4,224,128]{2,1,0:T(8,128)(2,1)S(1)} %pad_maximum_fusion.1.refs_4_), channel_id=1, source_target_pairs={{0,24},{8,16},{16,8},{24,0},{1,25},{9,17},{17,9},{25,1},{2,26},{10... | collective-permute-start | bytes 688136 | tf_op jit(solution)/shard_map/ppermute | solution.py:217
  50.8 0.1 collective-permute-start.14
  50.9 1.1 %collective-permute-start.13 = (bf16[4,224,128]{2,1,0:T(8,128)(2,1)S(1)}, bf16[4,224,128]{2,1,0:T(8,128)(2,1)S(1)}, u32[]{:S(2)}, u32[]{:S(2)}) collective-permute-start(bf16[4,224,128]{2,1,0:T(8,128)(2,1)S(1)} %pad_maximum_fusion.1.refs_4_), channel_id=1, source_target_pairs={{0,8},{8,0},{16,24},{24,16},{1,9},{9,1},{17,25},{25,17},{2,10},{10... | collective-permute-start | bytes 688136 | tf_op jit(solution)/shard_map/ppermute | solution.py:217
  52.1 1.6 %collective-permute-start.16 = (bf16[4,224,128]{2,1,0:T(8,128)(2,1)S(1)}, bf16[4,224,128]{2,1,0:T(8,128)(2,1)S(1)}, u32[]{:S(2)}, u32[]{:S(2)}) collective-permute-start(bf16[4,224,128]{2,1,0:T(8,128)(2,1)S(1)} %pad_maximum_fusion.1.refs_4_), channel_id=1, source_target_pairs={{0,1},{1,0},{2,3},{3,2},{4,5},{5,4},{6,7},{7,6},{8,9},{9,8},{10,11... | collective-permute-start | bytes 688136 | tf_op jit(solution)/shard_map/ppermute | solution.py:217
  53.6 3.2 %collective-permute-done.15.refs_7_ = bf16[4,224,128]{2,1,0:T(8,128)(2,1)S(1)} collective-permute-done((bf16[4,224,128]{2,1,0:T(8,128)(2,1)S(1)}, bf16[4,224,128]{2,1,0:T(8,128)(2,1)S(1)}, u32[]{:S(2)}, u32[]{:S(2)}) %collective-permute-start.15) | collective-permute-done | bytes 229408 | tf_op jit(solution)/shard_map/ppermute | solution.py:217
  56.8 2.7 %collective-permute-start.19 = (bf16[4,224,128]{2,1,0:T(8,128)(2,1)S(1)}, bf16[4,224,128]{2,1,0:T(8,128)(2,1)S(1)}, u32[]{:S(2)}, u32[]{:S(2)}) collective-permute-start(bf16[4,224,128]{2,1,0:T(8,128)(2,1)S(1)} %collective-permute-done.15.refs_7_), channel_id=1, source_target_pairs={{0,1},{1,0},{2,3},{3,2},{4,5},{5,4},{6,7},{7,6},{8,9},{9,8},{10,11... | collective-permute-start | bytes 688136 | tf_op jit(solution)/shard_map/ppermute | solution.py:217
  59.5 3.2 %collective-permute-done.14.refs_6_ = bf16[4,224,128]{2,1,0:T(8,128)(2,1)S(1)} collective-permute-done((bf16[4,224,128]{2,1,0:T(8,128)(2,1)S(1)}, bf16[4,224,128]{2,1,0:T(8,128)(2,1)S(1)}, u32[]{:S(2)}, u32[]{:S(2)}) %collective-permute-start.14) | collective-permute-done | bytes 229408 | tf_op jit(solution)/shard_map/ppermute | solution.py:217
  62.7 0.5 collective-permute-start.18
  63.2 0.3 collective-permute-start.17
  63.6 1.3 %moments.1.refs_3_ = bf16[128,640]{1,0:T(8,128)(2,1)S(1)} custom-call(bf16[8,128,192]{2,1,0:T(8,128)(2,1)S(1)} %get-tuple-element.13.table_ref, bf16[1536,128]{1,0:T(8,128)(2,1)S(1)} %get-tuple-element.14.w_out_ref.refs_1_), custom_call_target="tpu_custom_call" | custom-call | tf_op jit(solution)/shard_map/moments/pallas_call | solution.py:750
  65.0 7.3 %denoise.1 = f32[32,128]{1,0:T(8,128)S(1)} custom-call(s32[8]{0:T(128)S(1)} %copy-done.5, f32[64,512]{1,0:T(8,128)S(1)} %bitcast.31, f32[4,64,512]{2,1,0:T(8,128)S(1)} %bitcast.28, bf16[128,640]{1,0:T(8,128)(2,1)S(1)} %moments.1.refs_3_, bf16[4,224,128]{2,1,0:T(8,128)(2,1)S(1)} %pad_maximum_fusion.1.refs_4_, ...), custom_call_target="tpu_custom_call" | custom-call | tf_op jit(solution)/shard_map/denoise/pallas_call | solution.py:758
  72.3 1.5 %collective-permute-start.22 = (f32[32,128]{1,0:T(8,128)S(1)}, f32[32,128]{1,0:T(8,128)S(1)}, u32[]{:S(2)}, u32[]{:S(2)}) collective-permute-start(f32[32,128]{1,0:T(8,128)S(1)} %denoise.1), channel_id=1, source_target_pairs={{0,6},{1,7},{2,4},{3,5},{4,2},{5,3},{6,0},{7,1},{8,14},{9,15},{10,... | collective-permute-start | bytes 49160 | tf_op jit(solution)/shard_map/ppermute | solution.py:217
  73.8 2.1 %collective-permute-start.20 = (f32[32,128]{1,0:T(8,128)S(1)}, f32[32,128]{1,0:T(8,128)S(1)}, u32[]{:S(2)}, u32[]{:S(2)}) collective-permute-start(f32[32,128]{1,0:T(8,128)S(1)} %denoise.1), channel_id=1, source_target_pairs={{0,2},{1,3},{2,0},{3,1},{4,6},{5,7},{6,4},{7,5},{8,10},{9,11},{10,... | collective-permute-start | bytes 49160 | tf_op jit(solution)/shard_map/ppermute | solution.py:217
  75.9 0.8 collective-permute-done.22
  76.7 0.8 collective-permute-done.21
  77.6 1.3 %collective-permute-start.25 = (f32[4,32,128]{2,1,0:T(8,128)S(1)}, f32[4,32,128]{2,1,0:T(8,128)S(1)}, u32[]{:S(2)}, u32[]{:S(2)}) collective-permute-start(f32[4,32,128]{2,1,0:T(8,128)S(1)} %pad_maximum_fusion.3), channel_id=1, source_target_pairs={{0,24},{8,16},{16,8},{24,0},{1,25},{9,17},{17,9},{25,1},{2,26},{10... | collective-permute-start | bytes 196616 | tf_op jit(solution)/shard_map/ppermute | solution.py:217
  78.8 0.2 collective-permute-start.24
  79.1 1.2 %collective-permute-start.23 = (f32[4,32,128]{2,1,0:T(8,128)S(1)}, f32[4,32,128]{2,1,0:T(8,128)S(1)}, u32[]{:S(2)}, u32[]{:S(2)}) collective-permute-start(f32[4,32,128]{2,1,0:T(8,128)S(1)} %pad_maximum_fusion.3), channel_id=1, source_target_pairs={{0,8},{8,0},{16,24},{24,16},{1,9},{9,1},{17,25},{25,17},{2,10},{10... | collective-permute-start | bytes 196616 | tf_op jit(solution)/shard_map/ppermute | solution.py:217
  80.3 1.9 %collective-permute-done.23 = f32[4,32,128]{2,1,0:T(8,128)S(1)} collective-permute-done((f32[4,32,128]{2,1,0:T(8,128)S(1)}, f32[4,32,128]{2,1,0:T(8,128)S(1)}, u32[]{:S(2)}, u32[]{:S(2)}) %collective-permute-start.23) | collective-permute-done | bytes 65568 | tf_op jit(solution)/shard_map/ppermute | solution.py:217
  82.2 0.1 collective-permute-done.24
  82.4 3.0 %collective-permute-start.26 = (f32[16,32,128]{2,1,0:T(8,128)S(1)}, f32[16,32,128]{2,1,0:T(8,128)S(1)}, u32[]{:S(2)}, u32[]{:S(2)}) collective-permute-start(f32[16,32,128]{2,1,0:T(8,128)S(1)} %constant_dynamic-update-slice_fusion.refs_1_), channel_id=1, source_target_pairs={{0,1},{1,0},{2,3},{3,2},{4,5},{5,4},{6,7},{7,6},{8,9},{9,8},{10,11... | collective-permute-start | bytes 786440 | tf_op jit(solution)/shard_map/ppermute | solution.py:217
  85.4 1.2 %collective-permute-done.26.refs_2_ = f32[16,32,128]{2,1,0:T(8,128)S(1)} collective-permute-done((f32[16,32,128]{2,1,0:T(8,128)S(1)}, f32[16,32,128]{2,1,0:T(8,128)S(1)}, u32[]{:S(2)}, u32[]{:S(2)}) %collective-permute-start.26) | collective-permute-done | bytes 262176 | tf_op jit(solution)/shard_map/ppermute | solution.py:217
  86.6 9.5 %decode.1 = (f32[64,512]{1,0:T(8,128)}, bf16[16,2,16,512]{3,2,1,0:T(8,128)(2,1)}) custom-call(s32[32]{0:T(128)S(1)} %copy-done.6, f32[16,32,128]{2,1,0:T(8,128)S(1)} %constant_dynamic-update-slice_fusion.refs_1_, f32[16,32,128]{2,1,0:T(8,128)S(1)} %collective-permute-done.26.refs_2_, bf16[3,3,16,512]{3,2,1,0:T(8,128)(2,1)S(1)} %copy-done.2, ...), custom_call_target="tpu_custom_call" | custom-call | tf_op jit(solution)/shard_map/decode/pallas_call | solution.py:783
  (42 shorter events, 0.3 us)
Async XLA Ops:
  0.6 64.3 %copy-start.5 = (s32[8]{0:T(128)S(1)}, s32[8]{0:T(128)}, u32[]{:S(2)}) copy-start(s32[8]{0:T(128)} %refs_0_.4) | copy-start | bytes 100
  0.6 64.3 %copy-start = (f32[4,512,64]{1,2,0:T(8,128)S(1)}, f32[4,512,64]{1,2,0:T(8,128)}, u32[]{:S(2)}) copy-start(f32[4,512,64]{1,2,0:T(8,128)} %param.15) | copy-start | bytes 1572868
  0.7 64.3 %copy-start.3 = (f32[512,64]{0,1:T(8,128)S(1)}, f32[512,64]{0,1:T(8,128)}, u32[]{:S(2)}) copy-start(f32[512,64]{0,1:T(8,128)} %param.14) | copy-start | bytes 393220
  0.7 85.9 %slice-start = ((s8[4718592]{0:T(1024)(128)(4,1)}), s8[524288]{0:T(1024)(128)(4,1)S(1)}, s32[]{:S(2)}) async-start(s8[4718592]{0:T(1024)(128)(4,1)} %bitcast.26), calls=%async_computation | async-start | bytes 1048576
  3.7 4.4 %collective-permute-start.2 = (bf16[48,192]{1,0:T(8,128)(2,1)}, bf16[48,192]{1,0:T(8,128)(2,1)S(1)}, u32[]{:S(2)}, u32[]{:S(2)}) collective-permute-start(bf16[48,192]{1,0:T(8,128)(2,1)} %get-tuple-element.12), channel_id=1, source_target_pairs={{0,24},{8,16},{16,8},{24,0},{1,25},{9,17},{17,9},{25,1},{2,26},{10... | collective-permute-start | bytes 55304 | tf_op jit(solution)/shard_map/ppermute | solution.py:217
  6.7 2.9 %collective-permute-start.1 = (bf16[48,192]{1,0:T(8,128)(2,1)}, bf16[48,192]{1,0:T(8,128)(2,1)S(1)}, u32[]{:S(2)}, u32[]{:S(2)}) collective-permute-start(bf16[48,192]{1,0:T(8,128)(2,1)} %get-tuple-element.12), channel_id=1, source_target_pairs={{0,16},{8,24},{16,0},{24,8},{1,17},{9,25},{17,1},{25,9},{2,18},{10... | collective-permute-start | bytes 55304 | tf_op jit(solution)/shard_map/ppermute | solution.py:217
  6.9 2.9 %collective-permute-start = (bf16[48,192]{1,0:T(8,128)(2,1)}, bf16[48,192]{1,0:T(8,128)(2,1)S(1)}, u32[]{:S(2)}, u32[]{:S(2)}) collective-permute-start(bf16[48,192]{1,0:T(8,128)(2,1)} %get-tuple-element.12), channel_id=1, source_target_pairs={{0,8},{8,0},{16,24},{24,16},{1,9},{9,1},{17,25},{25,17},{2,10},{10... | collective-permute-start | bytes 55304 | tf_op jit(solution)/shard_map/ppermute | solution.py:217
  9.8 76.7 %copy-start.2 = (bf16[3,3,16,512]{3,2,1,0:T(8,128)(2,1)S(1)}, bf16[3,3,16,512]{3,2,1,0:T(8,128)(2,1)}, u32[]{:S(2)}) copy-start(bf16[3,3,16,512]{3,2,1,0:T(8,128)(2,1)} %refs_3_.3) | copy-start | bytes 442372
  9.8 76.7 %copy-start.4 = (f32[512]{0:T(512)S(1)}, f32[512]{0:T(512)}, u32[]{:S(2)}) copy-start(f32[512]{0:T(512)} %param.26) | copy-start | bytes 6148
  9.8 76.7 %copy-start.6 = (s32[32]{0:T(128)S(1)}, s32[32]{0:T(128)}, u32[]{:S(2)}) copy-start(s32[32]{0:T(128)} %refs_0_.5) | copy-start | bytes 388
  10.6 4.4 %collective-permute-start.4 = (bf16[4,48,192]{2,1,0:T(8,128)(2,1)S(1)}, bf16[4,48,192]{2,1,0:T(8,128)(2,1)S(1)}, u32[]{:S(2)}, u32[]{:S(2)}) collective-permute-start(bf16[4,48,192]{2,1,0:T(8,128)(2,1)S(1)} %get-tuple-element.23), channel_id=1, source_target_pairs={{0,4},{1,5},{2,6},{3,7},{4,0},{5,1},{6,2},{7,3},{8,12},{9,13},{10,... | collective-permute-start | bytes 221192 | tf_op jit(solution)/shard_map/ppermute | solution.py:217
  13.0 3.5 %collective-permute-start.3 = (bf16[4,48,192]{2,1,0:T(8,128)(2,1)S(1)}, bf16[4,48,192]{2,1,0:T(8,128)(2,1)S(1)}, u32[]{:S(2)}, u32[]{:S(2)}) collective-permute-start(bf16[4,48,192]{2,1,0:T(8,128)(2,1)S(1)} %get-tuple-element.23), channel_id=1, source_target_pairs={{0,2},{1,3},{2,0},{3,1},{4,6},{5,7},{6,4},{7,5},{8,10},{9,11},{10,... | collective-permute-start | bytes 221192 | tf_op jit(solution)/shard_map/ppermute | solution.py:217
  14.3 6.4 %collective-permute-start.5 = (bf16[4,48,192]{2,1,0:T(8,128)(2,1)S(1)}, bf16[4,48,192]{2,1,0:T(8,128)(2,1)S(1)}, u32[]{:S(2)}, u32[]{:S(2)}) collective-permute-start(bf16[4,48,192]{2,1,0:T(8,128)(2,1)S(1)} %get-tuple-element.23), channel_id=1, source_target_pairs={{0,6},{1,7},{2,4},{3,5},{4,2},{5,3},{6,0},{7,1},{8,14},{9,15},{10,... | collective-permute-start | bytes 221192 | tf_op jit(solution)/shard_map/ppermute | solution.py:217
  14.3 12.3 %collective-permute-start.7 = (bf16[1152,128]{1,0:T(8,128)(2,1)}, bf16[1152,128]{1,0:T(8,128)(2,1)S(1)}, u32[]{:S(2)}, u32[]{:S(2)}) collective-permute-start(bf16[1152,128]{1,0:T(8,128)(2,1)} %get-tuple-element.17), channel_id=1, source_target_pairs={{0,8},{8,0},{16,24},{24,16},{1,9},{9,1},{17,25},{25,17},{2,10},{10... | collective-permute-start | bytes 884744 | tf_op jit(solution)/shard_map/ppermute | solution.py:217
  20.7 4.5 %collective-permute-start.6 = (bf16[4,4,48,192]{3,2,1,0:T(8,128)(2,1)S(1)}, bf16[4,4,48,192]{3,2,1,0:T(8,128)(2,1)S(1)}, u32[]{:S(2)}, u32[]{:S(2)}) collective-permute-start(bf16[4,4,48,192]{3,2,1,0:T(8,128)(2,1)S(1)} %pad_maximum_fusion.refs_0_), channel_id=1, source_target_pairs={{0,1},{1,0},{2,3},{3,2},{4,5},{5,4},{6,7},{7,6},{8,9},{9,8},{10,11... | collective-permute-start | bytes 884744 | tf_op jit(solution)/shard_map/ppermute | solution.py:217
  23.8 15.0 %collective-permute-start.8 = (bf16[1152,128]{1,0:T(8,128)(2,1)}, bf16[1152,128]{1,0:T(8,128)(2,1)S(1)}, u32[]{:S(2)}, u32[]{:S(2)}) collective-permute-start(bf16[1152,128]{1,0:T(8,128)(2,1)} %get-tuple-element.18), channel_id=1, source_target_pairs={{0,16},{8,24},{16,0},{24,8},{1,17},{9,25},{17,1},{25,9},{2,18},{10... | collective-permute-start | bytes 884744 | tf_op jit(solution)/shard_map/ppermute | solution.py:217
  25.1 13.7 %collective-permute-start.9 = (bf16[1152,128]{1,0:T(8,128)(2,1)}, bf16[1152,128]{1,0:T(8,128)(2,1)S(1)}, u32[]{:S(2)}, u32[]{:S(2)}) collective-permute-start(bf16[1152,128]{1,0:T(8,128)(2,1)} %get-tuple-element.19), channel_id=1, source_target_pairs={{0,24},{8,16},{16,8},{24,0},{1,25},{9,17},{17,9},{25,1},{2,26},{10... | collective-permute-start | bytes 884744 | tf_op jit(solution)/shard_map/ppermute | solution.py:217
  38.8 1.0 %copy-start.1 = (bf16[1152,128]{1,0:T(8,128)(2,1)S(1)}, bf16[1152,128]{1,0:T(8,128)(2,1)}, u32[]{:S(2)}) copy-start(bf16[1152,128]{1,0:T(8,128)(2,1)} %get-tuple-element.16.refs_2_) | copy-start | bytes 884740
  39.8 46.8 %slice-start.1 = ((s8[4718592]{0:T(1024)(128)(4,1)}), s8[4194304]{0:T(1024)(128)(4,1)S(1)}, s32[]{:S(2)}) async-start(s8[4718592]{0:T(1024)(128)(4,1)} %bitcast.26), calls=%async_computation.1 | async-start | bytes 8388608
  41.0 5.0 %collective-permute-start.12 = (bf16[224,128]{1,0:T(8,128)(2,1)S(1)}, bf16[224,128]{1,0:T(8,128)(2,1)S(1)}, u32[]{:S(2)}, u32[]{:S(2)}) collective-permute-start(bf16[224,128]{1,0:T(8,128)(2,1)S(1)} %combine_weights.1), channel_id=1, source_target_pairs={{0,6},{1,7},{2,4},{3,5},{4,2},{5,3},{6,0},{7,1},{8,14},{9,15},{10,... | collective-permute-start | bytes 172040 | tf_op jit(solution)/shard_map/ppermute | solution.py:217
  42.9 6.4 %collective-permute-start.11 = (bf16[224,128]{1,0:T(8,128)(2,1)S(1)}, bf16[224,128]{1,0:T(8,128)(2,1)S(1)}, u32[]{:S(2)}, u32[]{:S(2)}) collective-permute-start(bf16[224,128]{1,0:T(8,128)(2,1)S(1)} %combine_weights.1), channel_id=1, source_target_pairs={{0,4},{1,5},{2,6},{3,7},{4,0},{5,1},{6,2},{7,3},{8,12},{9,13},{10,... | collective-permute-start | bytes 172040 | tf_op jit(solution)/shard_map/ppermute | solution.py:217
  43.1 6.2 %collective-permute-start.10 = (bf16[224,128]{1,0:T(8,128)(2,1)S(1)}, bf16[224,128]{1,0:T(8,128)(2,1)S(1)}, u32[]{:S(2)}, u32[]{:S(2)}) collective-permute-start(bf16[224,128]{1,0:T(8,128)(2,1)S(1)} %combine_weights.1), channel_id=1, source_target_pairs={{0,2},{1,3},{2,0},{3,1},{4,6},{5,7},{6,4},{7,5},{8,10},{9,11},{10,... | collective-permute-start | bytes 172040 | tf_op jit(solution)/shard_map/ppermute | solution.py:217
  49.3 7.5 %collective-permute-start.15 = (bf16[4,224,128]{2,1,0:T(8,128)(2,1)S(1)}, bf16[4,224,128]{2,1,0:T(8,128)(2,1)S(1)}, u32[]{:S(2)}, u32[]{:S(2)}) collective-permute-start(bf16[4,224,128]{2,1,0:T(8,128)(2,1)S(1)} %pad_maximum_fusion.1.refs_4_), channel_id=1, source_target_pairs={{0,24},{8,16},{16,8},{24,0},{1,25},{9,17},{17,9},{25,1},{2,26},{10... | collective-permute-start | bytes 688136 | tf_op jit(solution)/shard_map/ppermute | solution.py:217
  50.8 11.9 %collective-permute-start.14 = (bf16[4,224,128]{2,1,0:T(8,128)(2,1)S(1)}, bf16[4,224,128]{2,1,0:T(8,128)(2,1)S(1)}, u32[]{:S(2)}, u32[]{:S(2)}) collective-permute-start(bf16[4,224,128]{2,1,0:T(8,128)(2,1)S(1)} %pad_maximum_fusion.1.refs_4_), channel_id=1, source_target_pairs={{0,16},{8,24},{16,0},{24,8},{1,17},{9,25},{17,1},{25,9},{2,18},{10... | collective-permute-start | bytes 688136 | tf_op jit(solution)/shard_map/ppermute | solution.py:217
  50.9 12.3 %collective-permute-start.13 = (bf16[4,224,128]{2,1,0:T(8,128)(2,1)S(1)}, bf16[4,224,128]{2,1,0:T(8,128)(2,1)S(1)}, u32[]{:S(2)}, u32[]{:S(2)}) collective-permute-start(bf16[4,224,128]{2,1,0:T(8,128)(2,1)S(1)} %pad_maximum_fusion.1.refs_4_), channel_id=1, source_target_pairs={{0,8},{8,0},{16,24},{24,16},{1,9},{9,1},{17,25},{25,17},{2,10},{10... | collective-permute-start | bytes 688136 | tf_op jit(solution)/shard_map/ppermute | solution.py:217
  52.1 12.8 %collective-permute-start.16 = (bf16[4,224,128]{2,1,0:T(8,128)(2,1)S(1)}, bf16[4,224,128]{2,1,0:T(8,128)(2,1)S(1)}, u32[]{:S(2)}, u32[]{:S(2)}) collective-permute-start(bf16[4,224,128]{2,1,0:T(8,128)(2,1)S(1)} %pad_maximum_fusion.1.refs_4_), channel_id=1, source_target_pairs={{0,1},{1,0},{2,3},{3,2},{4,5},{5,4},{6,7},{7,6},{8,9},{9,8},{10,11... | collective-permute-start | bytes 688136 | tf_op jit(solution)/shard_map/ppermute | solution.py:217
  56.8 8.1 %collective-permute-start.19 = (bf16[4,224,128]{2,1,0:T(8,128)(2,1)S(1)}, bf16[4,224,128]{2,1,0:T(8,128)(2,1)S(1)}, u32[]{:S(2)}, u32[]{:S(2)}) collective-permute-start(bf16[4,224,128]{2,1,0:T(8,128)(2,1)S(1)} %collective-permute-done.15.refs_7_), channel_id=1, source_target_pairs={{0,1},{1,0},{2,3},{3,2},{4,5},{5,4},{6,7},{7,6},{8,9},{9,8},{10,11... | collective-permute-start | bytes 688136 | tf_op jit(solution)/shard_map/ppermute | solution.py:217
  62.7 2.2 %collective-permute-start.18 = (bf16[4,224,128]{2,1,0:T(8,128)(2,1)S(1)}, bf16[4,224,128]{2,1,0:T(8,128)(2,1)S(1)}, u32[]{:S(2)}, u32[]{:S(2)}) collective-permute-start(bf16[4,224,128]{2,1,0:T(8,128)(2,1)S(1)} %collective-permute-done.14.refs_6_), channel_id=1, source_target_pairs={{0,1},{1,0},{2,3},{3,2},{4,5},{5,4},{6,7},{7,6},{8,9},{9,8},{10,11... | collective-permute-start | bytes 688136 | tf_op jit(solution)/shard_map/ppermute | solution.py:217
  63.2 1.7 %collective-permute-start.17 = (bf16[4,224,128]{2,1,0:T(8,128)(2,1)S(1)}, bf16[4,224,128]{2,1,0:T(8,128)(2,1)S(1)}, u32[]{:S(2)}, u32[]{:S(2)}) collective-permute-start(bf16[4,224,128]{2,1,0:T(8,128)(2,1)S(1)} %collective-permute-done.13.refs_5_), channel_id=1, source_target_pairs={{0,1},{1,0},{2,3},{3,2},{4,5},{5,4},{6,7},{7,6},{8,9},{9,8},{10,11... | collective-permute-start | bytes 688136 | tf_op jit(solution)/shard_map/ppermute | solution.py:217
  72.3 4.5 %collective-permute-start.22 = (f32[32,128]{1,0:T(8,128)S(1)}, f32[32,128]{1,0:T(8,128)S(1)}, u32[]{:S(2)}, u32[]{:S(2)}) collective-permute-start(f32[32,128]{1,0:T(8,128)S(1)} %denoise.1), channel_id=1, source_target_pairs={{0,6},{1,7},{2,4},{3,5},{4,2},{5,3},{6,0},{7,1},{8,14},{9,15},{10,... | collective-permute-start | bytes 49160 | tf_op jit(solution)/shard_map/ppermute | solution.py:217
  73.8 3.8 %collective-permute-start.21 = (f32[32,128]{1,0:T(8,128)S(1)}, f32[32,128]{1,0:T(8,128)S(1)}, u32[]{:S(2)}, u32[]{:S(2)}) collective-permute-start(f32[32,128]{1,0:T(8,128)S(1)} %denoise.1), channel_id=1, source_target_pairs={{0,4},{1,5},{2,6},{3,7},{4,0},{5,1},{6,2},{7,3},{8,12},{9,13},{10,... | collective-permute-start | bytes 49160 | tf_op jit(solution)/shard_map/ppermute | solution.py:217
  73.8 3.8 %collective-permute-start.20 = (f32[32,128]{1,0:T(8,128)S(1)}, f32[32,128]{1,0:T(8,128)S(1)}, u32[]{:S(2)}, u32[]{:S(2)}) collective-permute-start(f32[32,128]{1,0:T(8,128)S(1)} %denoise.1), channel_id=1, source_target_pairs={{0,2},{1,3},{2,0},{3,1},{4,6},{5,7},{6,4},{7,5},{8,10},{9,11},{10,... | collective-permute-start | bytes 49160 | tf_op jit(solution)/shard_map/ppermute | solution.py:217
  77.6 4.8 %collective-permute-start.25 = (f32[4,32,128]{2,1,0:T(8,128)S(1)}, f32[4,32,128]{2,1,0:T(8,128)S(1)}, u32[]{:S(2)}, u32[]{:S(2)}) collective-permute-start(f32[4,32,128]{2,1,0:T(8,128)S(1)} %pad_maximum_fusion.3), channel_id=1, source_target_pairs={{0,24},{8,16},{16,8},{24,0},{1,25},{9,17},{17,9},{25,1},{2,26},{10... | collective-permute-start | bytes 196616 | tf_op jit(solution)/shard_map/ppermute | solution.py:217
  78.8 3.5 %collective-permute-start.24 = (f32[4,32,128]{2,1,0:T(8,128)S(1)}, f32[4,32,128]{2,1,0:T(8,128)S(1)}, u32[]{:S(2)}, u32[]{:S(2)}) collective-permute-start(f32[4,32,128]{2,1,0:T(8,128)S(1)} %pad_maximum_fusion.3), channel_id=1, source_target_pairs={{0,16},{8,24},{16,0},{24,8},{1,17},{9,25},{17,1},{25,9},{2,18},{10... | collective-permute-start | bytes 196616 | tf_op jit(solution)/shard_map/ppermute | solution.py:217
  79.1 3.1 %collective-permute-start.23 = (f32[4,32,128]{2,1,0:T(8,128)S(1)}, f32[4,32,128]{2,1,0:T(8,128)S(1)}, u32[]{:S(2)}, u32[]{:S(2)}) collective-permute-start(f32[4,32,128]{2,1,0:T(8,128)S(1)} %pad_maximum_fusion.3), channel_id=1, source_target_pairs={{0,8},{8,0},{16,24},{24,16},{1,9},{9,1},{17,25},{25,17},{2,10},{10... | collective-permute-start | bytes 196616 | tf_op jit(solution)/shard_map/ppermute | solution.py:217
  82.4 4.2 %collective-permute-start.26 = (f32[16,32,128]{2,1,0:T(8,128)S(1)}, f32[16,32,128]{2,1,0:T(8,128)S(1)}, u32[]{:S(2)}, u32[]{:S(2)}) collective-permute-start(f32[16,32,128]{2,1,0:T(8,128)S(1)} %constant_dynamic-update-slice_fusion.refs_1_), channel_id=1, source_target_pairs={{0,1},{1,0},{2,3},{3,2},{4,5},{5,4},{6,7},{7,6},{8,9},{9,8},{10,11... | collective-permute-start | bytes 786440 | tf_op jit(solution)/shard_map/ppermute | solution.py:217
